TPU v7x, 32 devices: a whole 2x2x4 slice. The times are simulated.
32 devices in a mesh: dp: 4 (over y, x), ctx: 8 (over z, core).
Axes of the slice: x: 2, y: 2, z: 4, core: 2. Of those that a mesh axis runs over, the one named last changes fastest.
Arguments:
- queries: bfloat16 [4096, 64, 128], P(('dp', 'ctx')), parts along dimension 0, may hold values from -4.5 to 4.5
- keys: bfloat16 [4096, 8, 128], P(('dp', 'ctx')), parts along dimension 0, may hold values from -4.5 to 4.5
- values: bfloat16 [4096, 8, 128], P(('dp', 'ctx')), parts along dimension 0, may hold values from -6 to 6
- out_grad: bfloat16 [4096, 64, 128], P(('dp', 'ctx')), parts along dimension 0, may hold values from -48 to 48
- rand_blocks: int32 [256, 16, 3], P(('dp', 'ctx')), parts along dimension 0, may hold values from 0 to 15, as said below
- global_blocks: int32 [8], P('dp'), parts along dimension 0, may hold values from 0 to 15, as said below
Outputs:
- output: bfloat16 [4096, 64, 128], P(('dp', 'ctx')), parts along dimension 0
- query_grad: bfloat16 [4096, 64, 128], P(('dp', 'ctx')), parts along dimension 0
- key_grad: bfloat16 [4096, 8, 128], P(('dp', 'ctx')), parts along dimension 0
- value_grad: bfloat16 [4096, 8, 128], P(('dp', 'ctx')), parts along dimension 0
There are 4 independent parts, one for each index of `dp`. A program takes and returns all parts, laid end to end along the dimension named above; each array names one. Nothing has to cross between parts.
Inputs may be any that keep to these rules, and one draw needn't show every extreme that they name: `rand_blocks`: for each query head and query block, 3 different blocks, none of them the query block or a block beside it (modulo 16), none of them a global block. `global_blocks`: 2 different blocks.
All inputs are finite; a program needn't handle non-finite values.
Results may differ from a plain program's by a relative error of at most 0.011.
Values may be sent and summed in bfloat16 or wider, within the bound.
A program may use at most 192 MiB of HBM per device.

v0:
```python
import functools
import math

import jax
import jax.numpy as jnp
from jax import lax
from jax.experimental import pallas as pl
from jax.experimental.pallas import tpu as pltpu
from jax.sharding import PartitionSpec as P

BLK = 64
NT = (((1,), (1,)), ((), ()))
NN = (((1,), (0,)), ((), ()))


def dot(left, right, dims=NN):
    return lax.dot_general(left, right, dims, preferred_element_type=jnp.float32)


def flat_rows(block):
    rows = block.shape[0] * block.shape[1]
    return block.astype(jnp.float32).reshape(rows, block.shape[2])


def for_chunks(count, step, init):
    return lax.fori_loop(0, count, step, init, unroll=count <= 4)


def attention(geometry, q_ref, g_ref, kv_ref, bias_ref, out_ref, dq_ref, dkv_ref, s_buf, e_buf, acc):
    chunk, row_tile = geometry
    shards, _, _, shard_tokens, width = kv_ref.shape
    length = shards * shard_tokens
    count = length // chunk
    tokens, group, _ = q_ref.shape
    rows = tokens * group
    tiles = rows // row_tile
    tile_tokens = row_tile // group
    factor = 1.0 / math.sqrt(width)
    to_log2 = factor * math.log2(math.e)
    per_chunk = chunk // shard_tokens

    def kv_chunk(which, c):
        return kv_ref[pl.ds(c * per_chunk, per_chunk), 0, which].reshape(chunk, width)

    for tile in range(tiles):
        t0 = tile * tile_tokens
        lanes = pl.ds(tile * row_tile, row_tile)
        q = flat_rows(q_ref[pl.ds(t0, tile_tokens)]).astype(jnp.bfloat16)
        g32 = flat_rows(g_ref[pl.ds(t0, tile_tokens)])

        def score_step(c, top):
            s = dot(kv_chunk(0, c), q, NT) * to_log2
            blocks = chunk // BLK
            bias = bias_ref[0, pl.ds(c * blocks, blocks), :, lanes]
            s = (s.reshape(blocks, BLK, row_tile) + bias).reshape(chunk, row_tile)
            s_buf[pl.ds(c * chunk, chunk)] = s
            return jnp.maximum(top, jnp.max(s, axis=0, keepdims=True))

        top = for_chunks(count, score_step, jnp.full((1, row_tile), -jnp.inf, jnp.float32))

        def weight_step(c, carry):
            total, out_t = carry
            e = jnp.exp2(s_buf[pl.ds(c * chunk, chunk)] - top)
            total = total + jnp.sum(e, axis=0, keepdims=True)
            e16 = e.astype(jnp.bfloat16)
            e_buf[pl.ds(c * chunk, chunk)] = e16
            out_t = out_t + dot(kv_chunk(1, c).T, e16)
            return total, out_t

        total, out_t = for_chunks(
            count,
            weight_step,
            (jnp.zeros((1, row_tile), jnp.float32), jnp.zeros((width, row_tile), jnp.float32)),
        )
        inverse = 1.0 / total
        out16 = (out_t * inverse).T.astype(jnp.bfloat16)
        out32 = out16.astype(jnp.float32)
        out_ref[pl.ds(t0, tile_tokens)] = out32.reshape(tile_tokens, group, width).astype(jnp.bfloat16)
        delta = jnp.sum((g32 * out32).T, axis=0, keepdims=True) * inverse
        g16 = (g32.T * inverse).T.astype(jnp.bfloat16)

        def grad_step(c, dq_t):
            at = pl.ds(c * chunk, chunk)
            e16 = e_buf[at]
            dp = dot(kv_chunk(1, c), g16, NT)
            ds = (e16.astype(jnp.float32) * (dp - delta)).astype(jnp.bfloat16)
            dk = dot(ds, q)
            dv = dot(e16, g16)
            if tile > 0:
                dk = dk + acc[0, at]
                dv = dv + acc[1, at]
            if tile < tiles - 1:
                acc[0, at] = dk
                acc[1, at] = dv
            else:
                shape = (per_chunk, shard_tokens, width)
                spot = pl.ds(c * per_chunk, per_chunk)
                dkv_ref[spot, 0, 0] = (dk * factor).astype(jnp.bfloat16).reshape(shape)
                dkv_ref[spot, 0, 1] = dv.astype(jnp.bfloat16).reshape(shape)
            return dq_t + dot(kv_chunk(0, c).T, ds)

        dq_t = for_chunks(count, grad_step, jnp.zeros((width, row_tile), jnp.float32))
        dq = (dq_t * factor).T.reshape(tile_tokens, group, width)
        dq_ref[pl.ds(t0, tile_tokens)] = dq.astype(jnp.bfloat16)


def local_attention(queries, out_grad, kv, bias):
    tokens, heads, width = queries.shape
    shards, kv_heads, _, shard_tokens, _ = kv.shape
    group = heads // kv_heads
    length = shards * shard_tokens
    rows = tokens * group
    chunk = math.gcd(length, 256)
    row_tile = rows
    while row_tile * length > (1 << 21) and row_tile > 128:
        row_tile //= 2
    acc_rows = length if row_tile < rows else 8
    blocks = length // BLK
    q_spec = pl.BlockSpec((tokens, group, width), lambda g: (0, g, 0))
    kv_spec = pl.BlockSpec((shards, 1, 2, shard_tokens, width), lambda g: (0, g, 0, 0, 0))
    return pl.pallas_call(
        functools.partial(attention, (chunk, row_tile)),
        grid=(kv_heads,),
        in_specs=[
            q_spec,
            q_spec,
            kv_spec,
            pl.BlockSpec((1, blocks, 1, rows), lambda g: (g, 0, 0, 0)),
        ],
        out_specs=[q_spec, q_spec, kv_spec],
        out_shape=[
            jax.ShapeDtypeStruct(queries.shape, jnp.bfloat16),
            jax.ShapeDtypeStruct(queries.shape, jnp.bfloat16),
            jax.ShapeDtypeStruct(kv.shape, jnp.bfloat16),
        ],
        scratch_shapes=[
            pltpu.VMEM((length, row_tile), jnp.float32),
            pltpu.VMEM((length, row_tile), jnp.bfloat16),
            pltpu.VMEM((2, acc_rows, width), jnp.float32),
        ],
        compiler_params=pltpu.CompilerParams(vmem_limit_bytes=60 * 1024 * 1024),
        name="attention",
    )(queries, out_grad, kv, bias)


def row_bias(rand_all, global_blocks, first, here, block_count, kv_heads):
    heads = rand_all.shape[0]
    group = heads // kv_heads
    mine = lax.dynamic_slice_in_dim(rand_all, first, here, axis=1)
    ids = first + jnp.arange(here, dtype=jnp.int32)
    key_ids = jnp.arange(block_count, dtype=jnp.int32)
    away = (key_ids[None, :] - ids[:, None] + block_count + 1) % block_count
    common = (away <= 2) | jnp.any(key_ids[None, :, None] == global_blocks[None, None, :], axis=2)
    chosen = jnp.any(mine[:, :, None, :] == key_ids[None, None, :, None], axis=3)
    live = chosen | common[None]
    bias = jnp.where(live, 0.0, -jnp.inf).astype(jnp.float32)
    bias = bias.reshape(kv_heads, group, here, block_count).transpose(0, 3, 2, 1)
    bias = jnp.broadcast_to(bias[:, :, :, None, :], (kv_heads, block_count, here, BLK, group))
    return bias.reshape(kv_heads, block_count, 1, here * BLK * group)


def fused_kernel(
    ids_in, k_in, v_in, q_hbm, g_hbm, out_hbm, dq_hbm, dk_ref, dv_ref, grads_ref,
    q_buf, g_buf, o_buf, dq_buf, kv_buf, part_buf, sib_in, right_in, left_in, right_out, left_out,
    ids_buf, bias_buf, s_buf, e_buf,
    q_sem, g_sem, o_sem, dq_sem,
    ids_send, ids_recv, sib_send, sib_recv, fwd_send, fwd_recv, back_send, back_recv,
    pair_send, pair_recv, right_send, right_recv, left_send, left_recv,
):
    heads, _, chips, _, shard_tokens, width = kv_buf.shape
    shards = 2 * chips
    _, tokens, group, _ = q_buf.shape
    rows = tokens * group
    here = tokens // BLK
    block_count = shards * here
    half = BLK * group
    factor = 1.0 / math.sqrt(width)
    to_log2 = factor * math.log2(math.e)
    me = lax.axis_index("ctx")
    z, core = me // 2, me % 2
    pair = z * 2 + 1 - core
    ahead, behind = me + 2, me - 2
    last = chips - 1

    def send(source, target, send_sem, recv_sem, to):
        return pltpu.make_async_remote_copy(
            src_ref=source, dst_ref=target, send_sem=send_sem, recv_sem=recv_sem,
            device_id={"ctx": to}, device_id_type=pl.DeviceIdType.MESH,
        )

    def send_ids(k):
        to = lax.rem(me + k, shards)
        return send(ids_in.at[to], ids_buf.at[me], ids_send.at[k], ids_recv.at[me], to)

    def got_ids(k):
        origin = lax.rem(me + k, shards)
        return send(ids_in.at[origin], ids_buf.at[origin], ids_send.at[k], ids_recv.at[origin], origin)

    def kv_move(h, origin, lane, sems, to):
        spot = kv_buf.at[h, lane, origin]
        return send(spot, spot, sems[0].at[h, origin], sems[1].at[h, origin], to)

    sib_sems, fwd_sems, back_sems = (sib_send, sib_recv), (fwd_send, fwd_recv), (back_send, back_recv)

    def pair_move(h):
        return send(part_buf.at[h, 1 - core], sib_in.at[h], pair_send.at[h], pair_recv.at[h], pair)

    def right_move(h, zd):
        return send(right_out.at[h, zd], right_in.at[h, zd], right_send.at[h, zd], right_recv.at[h, zd], ahead)

    def left_move(h, zd):
        return send(left_out.at[h, zd], left_in.at[h, zd], left_send.at[h, zd], left_recv.at[h, zd], behind)

    def head_columns(ref, h):
        return ref.at[:, pl.ds(pl.multiple_of(h * group, group), group), :]

    def load_q(h):
        return pltpu.make_async_copy(head_columns(q_hbm, h), q_buf.at[h], q_sem.at[h])

    def load_g(h):
        return pltpu.make_async_copy(head_columns(g_hbm, h), g_buf.at[h], g_sem.at[h])

    def store_o(h):
        return pltpu.make_async_copy(o_buf.at[h], head_columns(out_hbm, h), o_sem.at[h])

    def store_dq(h):
        return pltpu.make_async_copy(dq_buf.at[h], head_columns(dq_hbm, h), dq_sem.at[h])

    def each_head(step):
        def run(h, carry):
            step(h)
            return carry
        lax.fori_loop(0, heads, run, 0)

    def start_loads(h):
        load_q(h).start()
        load_g(h).start()

    each_head(start_loads)
    for which, ref in enumerate((k_in, v_in)):
        turned = jnp.swapaxes(ref[...].astype(jnp.float32), 0, 1)
        kv_buf[:, core, z, which] = turned.astype(jnp.bfloat16)
    ids_buf[me] = ids_in[me]

    barrier = pltpu.get_barrier_semaphore()
    for k in range(1, shards):
        pl.semaphore_signal(
            barrier, inc=1, device_id={"ctx": lax.rem(me + k, shards)}, device_id_type=pl.DeviceIdType.MESH
        )
    pl.semaphore_wait(barrier, shards - 1)

    def forward_kv(h, origin, rightward, leftward):
        @pl.when(rightward)
        def _():
            kv_move(h, origin, core, fwd_sems, ahead).start()

        @pl.when(leftward)
        def _():
            kv_move(h, origin, core, back_sems, behind).start()

        kv_move(h, origin, core, sib_sems, pair).start()

    def both(h):
        return part_buf[h, core].astype(jnp.float32), sib_in[h].astype(jnp.float32)

    def combined(h, zd):
        return part_buf[h, core, zd].astype(jnp.float32) + sib_in[h, zd].astype(jnp.float32)

    def in_heads(h):
        return jnp.logical_and(h >= 0, h < heads)

    def reduce_right(h):
        for zd in range(chips - 1, 0, -1):
            @pl.when(zd > z)
            def _(zd=zd):
                @pl.when(z == 0)
                def _():
                    right_out[h, zd] = combined(h, zd).astype(jnp.bfloat16)

                @pl.when(z > 0)
                def _():
                    right_move(h, zd).wait_recv()
                    total = combined(h, zd) + right_in[h, zd].astype(jnp.float32)
                    right_out[h, zd] = total.astype(jnp.bfloat16)

                right_move(h, zd).start()

    def reduce_left(h):
        for zd in range(chips - 1):
            @pl.when(zd < z)
            def _(zd=zd):
                @pl.when(z == last)
                def _():
                    left_out[h, zd] = combined(h, zd).astype(jnp.bfloat16)

                @pl.when(z < last)
                def _():
                    left_move(h, zd).wait_recv()
                    total = combined(h, zd) + left_in[h, zd].astype(jnp.float32)
                    left_out[h, zd] = total.astype(jnp.bfloat16)

                left_move(h, zd).start()

    def finish(h):
        @pl.when(z > 0)
        def _():
            right_move(h, z).wait_recv()

        @pl.when(z < last)
        def _():
            left_move(h, z).wait_recv()

        @pl.when(z == 0)
        def _():
            grads_ref[h] = (combined(h, z) + left_in[h, z].astype(jnp.float32)).astype(jnp.bfloat16)

        @pl.when(z == last)
        def _():
            grads_ref[h] = (combined(h, z) + right_in[h, z].astype(jnp.float32)).astype(jnp.bfloat16)

        @pl.when(jnp.logical_and(z > 0, z < last))
        def _():
            arrived = right_in[h, z].astype(jnp.float32) + left_in[h, z].astype(jnp.float32)
            grads_ref[h] = (combined(h, z) + arrived).astype(jnp.bfloat16)

    def compute(h):
        load_q(h).wait()
        load_g(h).wait()
        q = flat_rows(q_buf[h]).astype(jnp.bfloat16)
        g32 = flat_rows(g_buf[h])
        ids = ids_buf[h]
        key_ids = lax.broadcasted_iota(jnp.int32, (block_count, ids.shape[1]), 0)
        slots = (ids.shape[0] - 2) // here
        for b in range(here):
            away = key_ids - (me * here + b) + (block_count + 1)
            for _ in range(2):
                away = jnp.where(away >= block_count, away - block_count, away)
            live = (away <= 2) | (key_ids == ids[6:7]) | (key_ids == ids[7:8])
            for k in range(slots):
                live = live | (key_ids == ids[b * slots + k:b * slots + k + 1])
            bias = jnp.where(live, 0.0, -jnp.inf).astype(jnp.float32)
            reps = half // ids.shape[1]
            bias_buf[:, b * half:(b + 1) * half] = jnp.concatenate([bias] * reps, axis=1)

        chunk = 2 * shard_tokens
        spans = [(lane, zz) for lane in range(2) for zz in range(0, chips, 2)]

        def kv_chunk(which, span):
            return kv_buf[h, span[0], span[1]:span[1] + 2, which].reshape(chunk, width)

        top = None
        for c, span in enumerate(spans):
            s = dot(kv_chunk(0, span), q, NT) * to_log2
            pieces = []
            for j in range(2 * here):
                block = ((span[1] + j // here) * 2 + span[0]) * here + j % here
                pieces.append(s[j * BLK:(j + 1) * BLK] + bias_buf[block:block + 1])
            s = jnp.concatenate(pieces, axis=0)
            s_buf[c * chunk:(c + 1) * chunk] = s
            here_top = jnp.max(s, axis=0, keepdims=True)
            top = here_top if top is None else jnp.maximum(top, here_top)

        total = jnp.zeros((1, rows), jnp.float32)
        out_t = jnp.zeros((width, rows), jnp.float32)
        for c, span in enumerate(spans):
            e = jnp.exp2(s_buf[c * chunk:(c + 1) * chunk] - top)
            total = total + jnp.sum(e, axis=0, keepdims=True)
            e16 = e.astype(jnp.bfloat16)
            e_buf[c * chunk:(c + 1) * chunk] = e16
            out_t = out_t + dot(kv_chunk(1, span).T, e16)
        inverse = 1.0 / total
        out16 = (out_t * inverse).T.astype(jnp.bfloat16)
        out32 = out16.astype(jnp.float32)
        o_buf[h] = out32.reshape(tokens, group, width).astype(jnp.bfloat16)
        store_o(h).start()
        delta = jnp.sum((g32 * out32).T, axis=0, keepdims=True) * inverse
        g16 = (g32.T * inverse).T.astype(jnp.bfloat16)

        dq_t = jnp.zeros((width, rows), jnp.float32)
        for k, zz in [(k, zz) for k in range(2) for zz in range(0, chips, 2)]:
            if (k, zz) == (1, 0):
                pair_move(h).start()
            span = ((1 - core) if k == 0 else core, zz)
            start = pl.multiple_of((span[0] * (chips // 2) + zz // 2) * chunk, chunk)
            e16 = e_buf[pl.ds(start, chunk)]
            dp = dot(kv_chunk(1, span), g16, NT)
            ds = (e16.astype(jnp.float32) * (dp - delta)).astype(jnp.bfloat16)
            shape = (2, shard_tokens, width)
            dk = (dot(ds, q) * factor).astype(jnp.bfloat16)
            dv = dot(e16, g16).astype(jnp.bfloat16)
            part_buf[h, span[0], span[1]:span[1] + 2, 0] = dk.reshape(shape)
            part_buf[h, span[0], span[1]:span[1] + 2, 1] = dv.reshape(shape)
            dq_t = dq_t + dot(kv_chunk(0, span).T, ds)
        dq = (dq_t * factor).T.reshape(tokens, group, width)
        dq_buf[h] = dq.astype(jnp.bfloat16)
        store_dq(h).start()

    lag = chips - 1

    def slot(t, carry):
        for d in range(chips - 1, 0, -1):
            h = t - d

            @pl.when(in_heads(h))
            def _(h=h, d=d):
                @pl.when(z - d >= 0)
                def _():
                    kv_move(h, z - d, core, fwd_sems, ahead).wait_recv()
                    forward_kv(h, z - d, z < last, z < 0)

                @pl.when(z + d <= last)
                def _():
                    kv_move(h, z + d, core, back_sems, behind).wait_recv()
                    forward_kv(h, z + d, z < 0, z > 0)

        @pl.when(t < heads)
        def _():
            forward_kv(t, z, z < last, z > 0)

        @pl.when(t == 0)
        def _():
            for k in range(1, shards):
                send_ids(k).start()

        e = t - lag - 1

        @pl.when(in_heads(e))
        def _():
            pair_move(e).wait_recv()

        @pl.when(jnp.logical_and(in_heads(e - z), z < last))
        def _():
            reduce_right(e - z)

        @pl.when(jnp.logical_and(in_heads(e - (last - z)), z > 0))
        def _():
            reduce_left(e - (last - z))

        f = e - jnp.maximum(z, last - z)

        @pl.when(in_heads(f))
        def _():
            finish(f)

        @pl.when(t == lag)
        def _():
            for k in range(1, shards):
                got_ids(k).wait_recv()

        @pl.when(in_heads(t - lag))
        def _():
            for origin in range(chips):
                kv_move(t - lag, origin, 1 - core, sib_sems, pair).wait_recv()
            compute(t - lag)

        return carry

    lax.fori_loop(0, heads + lag + chips, slot, 0)

    for which, ref in enumerate((dk_ref, dv_ref)):
        turned = jnp.swapaxes(grads_ref[:, which].astype(jnp.float32), 0, 1)
        ref[...] = turned.astype(jnp.bfloat16)

    for k in range(1, shards):
        send_ids(k).wait_send()

    def drain(h):
        store_o(h).wait()
        store_dq(h).wait()
        pair_move(h).wait_send()
        for origin in range(chips):
            kv_move(h, origin, core, sib_sems, pair).wait_send()

            @pl.when(jnp.logical_and(origin <= z, z < last))
            def _(origin=origin):
                kv_move(h, origin, core, fwd_sems, ahead).wait_send()

            @pl.when(jnp.logical_and(origin >= z, z > 0))
            def _(origin=origin):
                kv_move(h, origin, core, back_sems, behind).wait_send()

            @pl.when(origin > z)
            def _(origin=origin):
                right_move(h, origin).wait_send()

            @pl.when(origin < z)
            def _(origin=origin):
                left_move(h, origin).wait_send()

    each_head(drain)


def fused(queries, out_grad, keys, values, ids):
    tokens, heads, width = queries.shape
    kv_heads = keys.shape[1]
    group = heads // kv_heads
    shards = ids.shape[0]
    chips = shards // 2
    rows = tokens * group
    length = tokens * shards
    bf16, f32 = jnp.bfloat16, jnp.float32
    vmem = pl.BlockSpec(memory_space=pltpu.VMEM)
    anywhere = pl.BlockSpec(memory_space=pl.ANY)
    dma = pltpu.SemaphoreType.DMA
    piece = (2, tokens, width)
    block = pltpu.VMEM((kv_heads, tokens, group, width), bf16)
    hop = pltpu.VMEM((kv_heads, chips) + piece, bf16)
    return pl.pallas_call(
        fused_kernel,
        in_specs=[vmem, vmem, vmem, anywhere, anywhere],
        out_specs=[anywhere, anywhere, vmem, vmem],
        out_shape=[
            jax.ShapeDtypeStruct(queries.shape, bf16),
            jax.ShapeDtypeStruct(queries.shape, bf16),
            jax.ShapeDtypeStruct(keys.shape, bf16),
            jax.ShapeDtypeStruct(keys.shape, bf16),
        ],
        scratch_shapes=[pltpu.VMEM((kv_heads,) + piece, bf16)] + [block] * 4
        + [pltpu.VMEM((kv_heads, 2, chips) + piece, bf16)] * 2
        + [hop] * 5
        + [
            pltpu.VMEM(ids.shape, jnp.int32),
            pltpu.VMEM((length // BLK, rows), f32),
            pltpu.VMEM((length, rows), f32),
            pltpu.VMEM((length, rows), bf16),
        ]
        + [dma((kv_heads,))] * 4
        + [dma((shards,))] * 2
        + [dma((kv_heads, chips))] * 6
        + [dma((kv_heads,))] * 2
        + [dma((kv_heads, chips))] * 4,
        compiler_params=pltpu.CompilerParams(
            collective_id=0, has_side_effects=True, vmem_limit_bytes=60 * 1024 * 1024
        ),
        name="fused",
    )(ids, keys, values, queries, out_grad)


def lane_ids(rand_blocks, global_blocks, shards, here):
    group, block_count, slots = rand_blocks.shape
    ids = rand_blocks.reshape(group, shards, here, slots).transpose(1, 2, 3, 0)
    ids = ids.reshape(shards, here * slots, 1, group)
    reps = 128 // group
    ids = jnp.broadcast_to(ids, (shards, here * slots, reps, group)).reshape(shards, here * slots, 128)
    common = jnp.broadcast_to(global_blocks[None, :, None], (shards, global_blocks.shape[0], 128))
    return jnp.concatenate([ids, common], axis=1)


def body(shards, queries, keys, values, out_grad, rand_blocks, global_blocks):
    tokens, kv_heads, width = keys.shape
    here = tokens // BLK
    block_count = rand_blocks.shape[1]
    group = queries.shape[1] // kv_heads
    me = lax.axis_index("ctx")
    if (shards == kv_heads == group == 8 and here == 2 and rand_blocks.shape[2] == 3
            and global_blocks.shape[0] == 2):
        ids = lane_ids(rand_blocks, global_blocks, shards, here)
        return fused(queries, out_grad, keys, values, ids)
    kv_here = jnp.stack([keys.transpose(1, 0, 2), values.transpose(1, 0, 2)], axis=1)
    kv = lax.all_gather(kv_here, "ctx", axis=0)
    rand_all = lax.all_gather(rand_blocks, "ctx", axis=0, tiled=True)
    bias = row_bias(rand_all, global_blocks, me * here, here, block_count, kv_heads)
    output, query_grad, parts = local_attention(queries, out_grad, kv, bias)
    sums = lax.psum_scatter(parts, "ctx", scatter_dimension=0, tiled=False)
    grads = sums.transpose(1, 2, 0, 3)
    return output, query_grad, grads[0], grads[1]


def solution(mesh):
    split = P(("dp", "ctx"), None, None)
    return jax.shard_map(
        functools.partial(body, mesh.shape["ctx"]),
        mesh=mesh,
        in_specs=(split, split, split, split, split, P("dp")),
        out_specs=(split, split, split, split),
        check_vma=False,
    )
```

profile of v0, /device:TPU:0, one launch (start us, length us, event | category | flops | bytes accessed | tf_op | source)
XLA Modules:
  0.0 88.8 jit_solution(15414850536884035890)
XLA Ops:
  0.6 0.7 pad.1.clone
  1.4 0.8 copy.10
  2.2 0.2 reshape.18
  2.4 0.7 pad_add_fusion.ids_in
  3.1 79.7 %fused.1 = (bf16[128,64,128]{2,1,0:T(8,128)(2,1)}, bf16[128,64,128]{2,1,0:T(8,128)(2,1)}, bf16[128,8,128]{2,1,0:T(8,128)(2,1)}, bf16[128,8,128]{2,1,0:T(8,128)(2,1)}) custom-call(s32[8,8,128]{2,1,0:T(8,128)} %pad_add_fusion.ids_in, bf16[128,8,128]{2,1,0:T(8,128)(2,1)} %k_in.1, bf16[128,8,128]{2,1,0:T(8,128)(2,1)} %v_in.1, bf16[128,64,128]{2,1,0:T(8,128)(2,1)} %q_hbm.1, ...), custom_call_target="tpu_custom_call" | custom-call | tf_op jit(solution)/shard_map/fused/pallas_call | solution.py:508
  82.8 0.0 copy-start
  82.8 3.2 %copy.17 = bf16[128,64,128]{2,1,0:T(8,128)(2,1)} copy(bf16[128,64,128]{2,1,0:T(8,128)(2,1)} %get-tuple-element.8) | data formatting | bytes 4194304
  86.0 0.0 copy-done
  86.0 0.0 copy-start.2
  86.0 0.0 copy-start.1
  86.0 1.3 %copy.18 = bf16[128,64,128]{2,1,0:T(8,128)(2,1)} copy(bf16[128,64,128]{2,1,0:T(8,128)(2,1)S(1)} %copy-done) | data formatting | bytes 4194304
  87.3 0.0 copy-done.2
  87.4 0.7 copy.19
  88.1 0.0 copy-done.1
  88.1 0.7 copy.20
  (3 shorter events, 0.0 us)
Async XLA Ops:
  82.8 3.2 %copy-start = (bf16[128,64,128]{2,1,0:T(8,128)(2,1)S(1)}, bf16[128,64,128]{2,1,0:T(8,128)(2,1)}, u32[]{:S(2)}) copy-start(bf16[128,64,128]{2,1,0:T(8,128)(2,1)} %get-tuple-element.9) | copy-start | bytes 6291460
  86.0 1.3 %copy-start.2 = (bf16[128,8,128]{2,1,0:T(8,128)(2,1)S(1)}, bf16[128,8,128]{2,1,0:T(8,128)(2,1)}, u32[]{:S(2)}) copy-start(bf16[128,8,128]{2,1,0:T(8,128)(2,1)} %get-tuple-element.10) | copy-start | bytes 786436
  86.0 2.0 %copy-start.1 = (bf16[128,8,128]{2,1,0:T(8,128)(2,1)S(1)}, bf16[128,8,128]{2,1,0:T(8,128)(2,1)}, u32[]{:S(2)}) copy-start(bf16[128,8,128]{2,1,0:T(8,128)(2,1)} %get-tuple-element.11) | copy-start | bytes 786436
where the time goes:
time: 89 us; the launch traced here: 88.8 us
  Pallas kernels  79.7 us (90%)
  local copies, waits for them, and re-layouts  7.72 us (9%)
    pallas_call x1, Pallas kernels, fused(): pl.pallas_call(fused_kernel, in_specs=[vmem, vmem, vmem, anywhere, anywhe...  79.7 us
    unnamed x11, local copies, waits for them, and re-layouts  6.74 us

commit v1 on v0

v1 whole, which is shorter than its diff:
```python
import functools
import math

import jax
import jax.numpy as jnp
from jax import lax
from jax.experimental import pallas as pl
from jax.experimental.pallas import tpu as pltpu
from jax.sharding import PartitionSpec as P

BLK = 64
NT = (((1,), (1,)), ((), ()))
NN = (((1,), (0,)), ((), ()))


def dot(left, right, dims=NN):
    return lax.dot_general(left, right, dims, preferred_element_type=jnp.float32)


def flat_rows(block):
    rows = block.shape[0] * block.shape[1]
    return block.astype(jnp.float32).reshape(rows, block.shape[2])


def for_chunks(count, step, init):
    return lax.fori_loop(0, count, step, init, unroll=count <= 4)


def attention(geometry, q_ref, g_ref, kv_ref, bias_ref, out_ref, dq_ref, dkv_ref, s_buf, e_buf, acc):
    chunk, row_tile = geometry
    shards, _, _, shard_tokens, width = kv_ref.shape
    length = shards * shard_tokens
    count = length // chunk
    tokens, group, _ = q_ref.shape
    rows = tokens * group
    tiles = rows // row_tile
    tile_tokens = row_tile // group
    factor = 1.0 / math.sqrt(width)
    to_log2 = factor * math.log2(math.e)
    per_chunk = chunk // shard_tokens

    def kv_chunk(which, c):
        return kv_ref[pl.ds(c * per_chunk, per_chunk), 0, which].reshape(chunk, width)

    for tile in range(tiles):
        t0 = tile * tile_tokens
        lanes = pl.ds(tile * row_tile, row_tile)
        q = flat_rows(q_ref[pl.ds(t0, tile_tokens)]).astype(jnp.bfloat16)
        g32 = flat_rows(g_ref[pl.ds(t0, tile_tokens)])

        def score_step(c, top):
            s = dot(kv_chunk(0, c), q, NT) * to_log2
            blocks = chunk // BLK
            bias = bias_ref[0, pl.ds(c * blocks, blocks), :, lanes]
            s = (s.reshape(blocks, BLK, row_tile) + bias).reshape(chunk, row_tile)
            s_buf[pl.ds(c * chunk, chunk)] = s
            return jnp.maximum(top, jnp.max(s, axis=0, keepdims=True))

        top = for_chunks(count, score_step, jnp.full((1, row_tile), -jnp.inf, jnp.float32))

        def weight_step(c, carry):
            total, out_t = carry
            e = jnp.exp2(s_buf[pl.ds(c * chunk, chunk)] - top)
            total = total + jnp.sum(e, axis=0, keepdims=True)
            e16 = e.astype(jnp.bfloat16)
            e_buf[pl.ds(c * chunk, chunk)] = e16
            out_t = out_t + dot(kv_chunk(1, c).T, e16)
            return total, out_t

        total, out_t = for_chunks(
            count,
            weight_step,
            (jnp.zeros((1, row_tile), jnp.float32), jnp.zeros((width, row_tile), jnp.float32)),
        )
        inverse = 1.0 / total
        out16 = (out_t * inverse).T.astype(jnp.bfloat16)
        out32 = out16.astype(jnp.float32)
        out_ref[pl.ds(t0, tile_tokens)] = out32.reshape(tile_tokens, group, width).astype(jnp.bfloat16)
        delta = jnp.sum((g32 * out32).T, axis=0, keepdims=True) * inverse
        g16 = (g32.T * inverse).T.astype(jnp.bfloat16)

        def grad_step(c, dq_t):
            at = pl.ds(c * chunk, chunk)
            e16 = e_buf[at]
            dp = dot(kv_chunk(1, c), g16, NT)
            ds = (e16.astype(jnp.float32) * (dp - delta)).astype(jnp.bfloat16)
            dk = dot(ds, q)
            dv = dot(e16, g16)
            if tile > 0:
                dk = dk + acc[0, at]
                dv = dv + acc[1, at]
            if tile < tiles - 1:
                acc[0, at] = dk
                acc[1, at] = dv
            else:
                shape = (per_chunk, shard_tokens, width)
                spot = pl.ds(c * per_chunk, per_chunk)
                dkv_ref[spot, 0, 0] = (dk * factor).astype(jnp.bfloat16).reshape(shape)
                dkv_ref[spot, 0, 1] = dv.astype(jnp.bfloat16).reshape(shape)
            return dq_t + dot(kv_chunk(0, c).T, ds)

        dq_t = for_chunks(count, grad_step, jnp.zeros((width, row_tile), jnp.float32))
        dq = (dq_t * factor).T.reshape(tile_tokens, group, width)
        dq_ref[pl.ds(t0, tile_tokens)] = dq.astype(jnp.bfloat16)


def local_attention(queries, out_grad, kv, bias):
    tokens, heads, width = queries.shape
    shards, kv_heads, _, shard_tokens, _ = kv.shape
    group = heads // kv_heads
    length = shards * shard_tokens
    rows = tokens * group
    chunk = math.gcd(length, 256)
    row_tile = rows
    while row_tile * length > (1 << 21) and row_tile > 128:
        row_tile //= 2
    acc_rows = length if row_tile < rows else 8
    blocks = length // BLK
    q_spec = pl.BlockSpec((tokens, group, width), lambda g: (0, g, 0))
    kv_spec = pl.BlockSpec((shards, 1, 2, shard_tokens, width), lambda g: (0, g, 0, 0, 0))
    return pl.pallas_call(
        functools.partial(attention, (chunk, row_tile)),
        grid=(kv_heads,),
        in_specs=[
            q_spec,
            q_spec,
            kv_spec,
            pl.BlockSpec((1, blocks, 1, rows), lambda g: (g, 0, 0, 0)),
        ],
        out_specs=[q_spec, q_spec, kv_spec],
        out_shape=[
            jax.ShapeDtypeStruct(queries.shape, jnp.bfloat16),
            jax.ShapeDtypeStruct(queries.shape, jnp.bfloat16),
            jax.ShapeDtypeStruct(kv.shape, jnp.bfloat16),
        ],
        scratch_shapes=[
            pltpu.VMEM((length, row_tile), jnp.float32),
            pltpu.VMEM((length, row_tile), jnp.bfloat16),
            pltpu.VMEM((2, acc_rows, width), jnp.float32),
        ],
        compiler_params=pltpu.CompilerParams(vmem_limit_bytes=60 * 1024 * 1024),
        name="attention",
    )(queries, out_grad, kv, bias)


def row_bias(rand_all, global_blocks, first, here, block_count, kv_heads):
    heads = rand_all.shape[0]
    group = heads // kv_heads
    mine = lax.dynamic_slice_in_dim(rand_all, first, here, axis=1)
    ids = first + jnp.arange(here, dtype=jnp.int32)
    key_ids = jnp.arange(block_count, dtype=jnp.int32)
    away = (key_ids[None, :] - ids[:, None] + block_count + 1) % block_count
    common = (away <= 2) | jnp.any(key_ids[None, :, None] == global_blocks[None, None, :], axis=2)
    chosen = jnp.any(mine[:, :, None, :] == key_ids[None, None, :, None], axis=3)
    live = chosen | common[None]
    bias = jnp.where(live, 0.0, -jnp.inf).astype(jnp.float32)
    bias = bias.reshape(kv_heads, group, here, block_count).transpose(0, 3, 2, 1)
    bias = jnp.broadcast_to(bias[:, :, :, None, :], (kv_heads, block_count, here, BLK, group))
    return bias.reshape(kv_heads, block_count, 1, here * BLK * group)


def fused_kernel(
    rand_in, glob_in, k_in, v_in, q_hbm, g_hbm, out_ref, dq_ref, dk_ref, dv_ref,
    grads_ref, q_buf, g_buf, kv_buf, part_buf, sib_in, right_in, left_in, right_out, left_out,
    ids_out, ids_buf, bias_buf, s_buf, e_buf, ds_buf, vt_buf, kt_buf, qt_buf, gt_buf,
    q_sem, g_sem,
    ids_send, sib_send, fwd_send, back_send, pair_send, right_send, left_send,
    ids_recv, sib_recv, kv_recv, pair_recv, right_recv, left_recv,
):
    heads, _, chips, _, shard_tokens, width = kv_buf.shape
    shards = 2 * chips
    _, tokens, group, _ = q_buf.shape
    rows = tokens * group
    here = tokens // BLK
    block_count = shards * here
    lane_keys = chips * shard_tokens
    tile = 256
    tiles = rows // tile
    tile_tokens = tile // group
    chunk = 2 * shard_tokens
    chunks = shards * shard_tokens // chunk
    factor = 1.0 / math.sqrt(width)
    to_log2 = factor * math.log2(math.e)
    me = lax.axis_index("ctx")
    z, core = me // 2, me % 2
    pair = z * 2 + 1 - core
    ahead, behind = me + 2, me - 2
    last = chips - 1

    barrier = pltpu.get_barrier_semaphore()
    for k in range(1, shards):
        pl.semaphore_signal(
            barrier, inc=1, device_id={"ctx": lax.rem(me + k, shards)}, device_id_type=pl.DeviceIdType.MESH
        )

    def send(source, target, send_sem, recv_sem, to):
        return pltpu.make_async_remote_copy(
            src_ref=source, dst_ref=target, send_sem=send_sem, recv_sem=recv_sem,
            device_id={"ctx": to}, device_id_type=pl.DeviceIdType.MESH,
        )

    def send_ids(k):
        to = lax.rem(me + k, shards)
        return send(ids_out.at[to], ids_buf.at[me], ids_send, ids_recv.at[me], to)

    def got_ids(k):
        origin = lax.rem(me + k, shards)
        return send(ids_out.at[origin], ids_buf.at[origin], ids_send, ids_recv.at[origin], origin)

    def kv_move(h, origin, send_sem, to):
        spot = kv_buf.at[h, core, origin]
        return send(spot, spot, send_sem, kv_recv.at[h, origin], to)

    def right_kv(h, origin):
        return kv_move(h, origin, fwd_send, ahead)

    def left_kv(h, origin):
        return kv_move(h, origin, back_send, behind)

    def sib_kv(h, origin):
        spot = kv_buf.at[h, core, origin]
        return send(spot, spot, sib_send, sib_recv.at[h], pair)

    def pair_move(h, w):
        return send(part_buf.at[h, w, 1 - core], sib_in.at[h, w], pair_send, pair_recv.at[h, w], pair)

    def side_move(side, h, w, zd):
        if side == 0:
            return send(right_out.at[h, w, zd], right_in.at[h, w, zd], right_send, right_recv.at[h, w, zd], ahead)
        return send(left_out.at[h, w, zd], left_in.at[h, w, zd], left_send, left_recv.at[h, w, zd], behind)

    def head_columns(ref, h):
        return ref.at[:, pl.ds(pl.multiple_of(h * group, group), group), :]

    def load_q(h):
        return pltpu.make_async_copy(head_columns(q_hbm, h), q_buf.at[h], q_sem.at[h])

    def load_g(h):
        return pltpu.make_async_copy(head_columns(g_hbm, h), g_buf.at[h], g_sem.at[h])

    def each_head(step):
        def run(h, carry):
            step(h)
            return carry
        lax.fori_loop(0, heads, run, 0)

    for which, ref in enumerate((k_in, v_in)):
        turned = jnp.swapaxes(ref[...].astype(jnp.float32), 0, 1)
        kv_buf[:, core, z, which] = turned.astype(jnp.bfloat16)

    slots = rand_in.shape[0]
    lanes = ids_buf.shape[2]
    spread = lax.broadcasted_iota(jnp.int32, (group, lanes), 1) % group
    spread = (spread == lax.broadcasted_iota(jnp.int32, (group, lanes), 0)).astype(jnp.float32)
    for k in range(slots):
        picks = lax.dot_general(
            rand_in[k].astype(jnp.float32), spread, (((0,), (0,)), ((), ())), preferred_element_type=jnp.float32
        )
        for to in range(shards):
            for b in range(here):
                spot = to * here + b
                ids_out[to, b * slots + k:b * slots + k + 1] = picks[spot:spot + 1]
    ids_buf[me] = ids_out[me]

    pl.semaphore_wait(barrier, shards - 1)

    def own_right(h):
        @pl.when(z < last)
        def _():
            right_kv(h, z).start()

    def own_left(h):
        @pl.when(z > 0)
        def _():
            left_kv(h, z).start()

    def own_sib(h):
        sib_kv(h, z).start()

    def arrive(h, distance):
        for zz in range(chips):
            @pl.when(jnp.logical_and(z == zz, h < heads))
            def _(zz=zz):
                for origin in (zz - distance, zz + distance):
                    if origin < 0 or origin > last:
                        continue
                    kv_move(h, origin, fwd_send, pair).wait_recv()
                    if origin < zz < last:
                        right_kv(h, origin).start()
                    if 0 < zz < origin:
                        left_kv(h, origin).start()
                    sib_kv(h, origin).start()

    def over(low, high, step):
        def run(h, carry):
            step(h)
            return carry
        lax.fori_loop(low, high, run, 0)

    def combined(h, w, zd):
        return part_buf[h, w, core, zd].astype(jnp.float32) + sib_in[h, w, zd].astype(jnp.float32)

    def reduce(rank, h, w):
        for side in range(2):
            zz = rank if side == 0 else last - rank
            targets = range(last, zz, -1) if side == 0 else range(zz)
            out, arrived = (right_out, right_in) if side == 0 else (left_out, left_in)

            @pl.when(jnp.logical_and(z == zz, h >= 0))
            def _(side=side, targets=targets, out=out, arrived=arrived):
                for zd in targets:
                    total = combined(h, w, zd)
                    if rank > 0:
                        side_move(side, h, w, zd).wait_recv()
                        total = total + arrived[h, w, zd].astype(jnp.float32)
                    out[h, w, zd] = total.astype(jnp.bfloat16)
                    side_move(side, h, w, zd).start()

    def finish(h, w):
        for zz in range(chips):
            @pl.when(z == zz)
            def _(zz=zz):
                total = combined(h, w, zz)
                if zz > 0:
                    side_move(0, h, w, zz).wait_recv()
                    total = total + right_in[h, w, zz].astype(jnp.float32)
                if zz < last:
                    side_move(1, h, w, zz).wait_recv()
                    total = total + left_in[h, w, zz].astype(jnp.float32)
                grads_ref[h, w] = total.T.astype(jnp.bfloat16)

    def compute(h, hooks):
        load_q(h).wait()
        load_g(h).wait()
        ids = ids_buf[h]
        key_ids = lax.broadcasted_iota(jnp.int32, (block_count, lanes), 0)
        key_float = key_ids.astype(jnp.float32)
        for b in range(here):
            away = key_ids - (me * here + b) + (block_count + 1)
            for _ in range(2):
                away = jnp.where(away >= block_count, away - block_count, away)
            live = (away <= 2) | (key_ids == glob_in[0]) | (key_ids == glob_in[1])
            for k in range(slots):
                live = live | (key_float == ids[b * slots + k:b * slots + k + 1])
            bias = jnp.where(live, 0.0, -jnp.inf).astype(jnp.float32)
            for block in range(block_count):
                bias_buf[b * block_count + block] = jnp.broadcast_to(bias[block:block + 1], (8, lanes))

        def key_rows(which, c):
            lane, zz = c * chunk // lane_keys, c * chunk % lane_keys // shard_tokens
            return kv_buf[h, lane, zz:zz + 2, which].reshape(chunk, width)

        def columns(r):
            return slice(r * tile, (r + 1) * tile)

        def keys_at(c):
            return slice(c * chunk, (c + 1) * chunk)

        def turned_rows(ref, r):
            return ref[h, r * tile_tokens:(r + 1) * tile_tokens].reshape(tile, width).T

        def put_rows(ref, r, turned):
            block = turned.T.reshape(tile_tokens, group, width)
            ref[r * tile_tokens:(r + 1) * tile_tokens, pl.ds(pl.multiple_of(h * group, group), group), :] = block

        tops, totals, deltas = {}, {}, {}

        def turn_keys(which, ref):
            for c in range(chunks):
                ref[:, keys_at(c)] = key_rows(which, c).T

        def scores(r):
            qt = turned_rows(q_buf, r)
            qt_buf[:, columns(r)] = qt
            b = r * tile // (rows // here)
            top = None
            for c in range(chunks):
                lane, zz = c * chunk // lane_keys, c * chunk % lane_keys // shard_tokens
                s = dot(key_rows(0, c), qt)
                for j in range(chunk // BLK):
                    block = ((zz + j // here) * 2 + lane) * here + j % here
                    bias = bias_buf[b * block_count + block]
                    bias = jnp.concatenate([bias] * (tile // lanes), axis=1)
                    piece = s[j * BLK:(j + 1) * BLK].reshape(BLK // 8, 8, tile) + bias[None]
                    at = c * chunk + j * BLK
                    s_buf[at:at + BLK, columns(r)] = piece.reshape(BLK, tile)
                    high = jnp.max(piece, axis=0)
                    top = high if top is None else jnp.maximum(top, high)
            tops[r] = jnp.max(top, axis=0, keepdims=True) * to_log2

        def weights(r):
            total = jnp.zeros((8, tile), jnp.float32)
            for c in range(chunks):
                e = jnp.exp2(s_buf[keys_at(c), columns(r)] * to_log2 - tops[r])
                total = total + jnp.sum(e.reshape(chunk // 8, 8, tile), axis=0)
                e_buf[keys_at(c), columns(r)] = e.astype(jnp.bfloat16)
            totals[r] = jnp.sum(total, axis=0, keepdims=True)

        def outputs(r):
            out_t = dot(vt_buf[...], e_buf[:, columns(r)])
            inverse = 1.0 / totals[r]
            out16 = (out_t * inverse).astype(jnp.bfloat16)
            gt = turned_rows(g_buf, r).astype(jnp.float32)
            deltas[r] = jnp.sum(gt * out16.astype(jnp.float32), axis=0, keepdims=True) * inverse
            gt_buf[:, columns(r)] = (gt * inverse).astype(jnp.bfloat16)
            put_rows(out_ref, r, out16)

        def score_grads(r):
            gt = gt_buf[:, columns(r)]
            for c in range(chunks):
                dp = dot(key_rows(1, c), gt)
                e = e_buf[keys_at(c), columns(r)].astype(jnp.float32)
                ds_buf[keys_at(c), columns(r)] = (e * (dp - deltas[r])).astype(jnp.bfloat16)

        def query_grads(r):
            dq_t = dot(kt_buf[...], ds_buf[:, columns(r)]) * factor
            put_rows(dq_ref, r, dq_t.astype(jnp.bfloat16))

        def key_grads(lane, w):
            left, right = ((qt_buf, ds_buf), (gt_buf, e_buf))[w]
            for zz in range(0, chips, 2):
                at = pl.ds(pl.multiple_of(lane * lane_keys + zz * shard_tokens, chunk), chunk)
                grad = dot(left[...], right[at], NT)
                if w == 0:
                    grad = grad * factor
                grad = grad.astype(jnp.bfloat16)
                for j in range(2):
                    part_buf[h, w, lane, zz + j] = grad[:, j * shard_tokens:(j + 1) * shard_tokens]

        turn_keys(1, vt_buf)
        scores(0)
        scores(1)
        weights(0)
        scores(2)
        weights(1)
        outputs(0)
        hooks[0]()
        scores(3)
        weights(2)
        outputs(1)
        turn_keys(0, kt_buf)
        weights(3)
        outputs(2)
        outputs(3)
        hooks[1]()
        key_grads(1 - core, 1)
        score_grads(0)
        score_grads(1)
        pair_move(h, 1).start()
        hooks[2]()
        score_grads(2)
        score_grads(3)
        key_grads(1 - core, 0)
        pair_move(h, 0).start()
        hooks[3]()
        key_grads(core, 1)
        key_grads(core, 0)
        for r in range(tiles):
            query_grads(r)
        hooks[4]()

    def lead(rank, t):
        return jnp.where(rank == 0, heads, jnp.minimum(jnp.where(rank == 1, 3 + 2 * t, 2 + t), heads))

    def start_loads(h):
        load_q(h).start()
        load_g(h).start()

    own_right(0)
    own_left(0)
    for h in range(3):
        own_sib(h)
    for k in range(1, shards):
        send_ids(k).start()
    each_head(start_loads)
    arrive(0, 1)
    over(1, lead(z, 0), own_right)
    over(1, lead(last - z, 0), own_left)
    for distance in range(2, chips):
        arrive(0, distance)
    ends = jnp.logical_or(z == 0, z == last)
    middle = jnp.logical_not(ends)

    @pl.when(middle)
    def _():
        arrive(1, 1)

    for k in range(1, shards):
        got_ids(k).wait_recv()

    def slot(t, carry):
        over(lead(z, t), lead(z, t + 1), own_right)
        over(lead(last - z, t), lead(last - z, t + 1), own_left)

        @pl.when(t + 3 < heads)
        def _():
            own_sib(t + 3)

        send(kv_buf.at[t, 1 - core], kv_buf.at[t, 1 - core], sib_send, sib_recv.at[t], pair).wait_recv()

        def end_arrive(distance):
            @pl.when(ends)
            def _():
                arrive(t + 1, distance)

        def middle_arrive(*events):
            for when, h, distance in events:
                @pl.when(jnp.logical_and(middle, when))
                def _(h=h, distance=distance):
                    arrive(h, distance)

        def caught(rank_lag):
            low = jnp.where(t == heads - 2, 0, t - rank_lag)
            return low, jnp.where(t < heads - 2, low, t - rank_lag + 1)

        def far(w, rank_lag):
            low, high = caught(rank_lag)
            over(low, high, lambda h: reduce(2, h, w))

        def hook0():
            @pl.when(t > 0)
            def _():
                pair_move(t - 1, 0).wait_recv()
                reduce(0, t - 1, 0)
            end_arrive(1)
            middle_arrive((t == 0, 2, 1), (t == 0, 1, 2))

        def hook1():
            reduce(1, t - 1, 1)
            far(0, 2)
            end_arrive(2)
            middle_arrive((t == 1, 4, 1), (t == 3, 7, 1))

        def hook2():
            end_arrive(3)
            middle_arrive((t == 2, 6, 1), (t > 0, t + 2, 2))

        def hook3():
            middle_arrive((t == 0, 3, 1))

        def hook4():
            pair_move(t, 1).wait_recv()
            reduce(0, t, 1)
            reduce(1, t - 1, 0)
            far(1, 1)
            middle_arrive((t == 0, 2, 2), (t == 1, 5, 1))

        compute(t, [hook0, hook1, hook2, hook3, hook4])
        return carry

    lax.fori_loop(0, heads, slot, 0)

    final = heads - 1

    def finish_both(h):
        finish(h, 1)
        finish(h, 0)

    reduce(2, final - 1, 0)
    reduce(1, final, 1)
    reduce(2, final, 1)
    pair_move(final, 0).wait_recv()
    reduce(0, final, 0)
    over(0, 2, finish_both)
    reduce(1, final, 0)
    over(2, 5, finish_both)
    reduce(2, final, 0)
    over(5, heads, finish_both)

    for which, ref in enumerate((dk_ref, dv_ref)):
        turned = jnp.swapaxes(grads_ref[:, which].astype(jnp.float32), 0, 1)
        ref[...] = turned.astype(jnp.bfloat16)

    def drained(region, sem):
        send(region, region, sem, ids_recv.at[0], pair).wait_send()

    drained(ids_out.at[pl.ds(1, shards - 1)], ids_send)
    drained(kv_buf.at[:, 0], sib_send)
    drained(sib_in, pair_send)
    for zz in range(chips):
        @pl.when(z == zz)
        def _(zz=zz):
            if zz < last:
                drained(kv_buf.at[:, 0, pl.ds(0, zz + 1)], fwd_send)
                drained(right_out.at[:, :, pl.ds(0, last - zz)], right_send)
            if zz > 0:
                drained(kv_buf.at[:, 0, pl.ds(0, chips - zz)], back_send)
                drained(left_out.at[:, :, pl.ds(0, zz)], left_send)


def fused(queries, out_grad, keys, values, rand_blocks, global_blocks, shards):
    tokens, heads, width = queries.shape
    kv_heads = keys.shape[1]
    group = heads // kv_heads
    chips = shards // 2
    rows = tokens * group
    length = tokens * shards
    blocks = length // BLK
    here = tokens // BLK
    bf16, f32 = jnp.bfloat16, jnp.float32
    vmem = pl.BlockSpec(memory_space=pltpu.VMEM)
    smem = pl.BlockSpec(memory_space=pltpu.SMEM)
    anywhere = pl.BlockSpec(memory_space=pl.ANY)
    dma = pltpu.SemaphoreType.DMA
    piece = (2, tokens, width)
    block = pltpu.VMEM((kv_heads, tokens, group, width), bf16)
    hop = pltpu.VMEM((kv_heads, 2, chips, width, tokens), bf16)
    results = pl.pallas_call(
        fused_kernel,
        in_specs=[vmem, smem, vmem, vmem, anywhere, anywhere],
        out_specs=[vmem] * 4,
        out_shape=[
            pltpu.VMEM(queries.shape, bf16),
            pltpu.VMEM(queries.shape, bf16),
            pltpu.VMEM(keys.shape, bf16),
            pltpu.VMEM(keys.shape, bf16),
        ],
        scratch_shapes=[pltpu.VMEM((kv_heads,) + piece, bf16)] + [block] * 2
        + [
            pltpu.VMEM((kv_heads, 2, chips) + piece, bf16),
            pltpu.VMEM((kv_heads, 2, 2, chips, width, tokens), bf16),
        ]
        + [hop] * 5
        + [
            pltpu.VMEM((shards, 8, 128), f32),
            pltpu.VMEM((shards, 8, 128), f32),
            pltpu.VMEM((here * blocks, 8, 128), f32),
            pltpu.VMEM((length, rows), f32),
            pltpu.VMEM((length, rows), bf16),
            pltpu.VMEM((length, rows), bf16),
            pltpu.VMEM((width, length), bf16),
            pltpu.VMEM((width, length), bf16),
            pltpu.VMEM((width, rows), bf16),
            pltpu.VMEM((width, rows), bf16),
        ]
        + [dma((kv_heads,))] * 2
        + [dma] * 7
        + [dma((shards,)), dma((kv_heads,)), dma((kv_heads, chips)), dma((kv_heads, 2))]
        + [dma((kv_heads, 2, chips))] * 2,
        compiler_params=pltpu.CompilerParams(
            collective_id=0, has_side_effects=True, vmem_limit_bytes=50 * 1024 * 1024
        ),
        name="fused",
    )(rand_blocks.transpose(2, 0, 1), global_blocks, keys, values, queries, out_grad)
    return results


def body(shards, queries, keys, values, out_grad, rand_blocks, global_blocks):
    tokens, kv_heads, width = keys.shape
    here = tokens // BLK
    block_count = rand_blocks.shape[1]
    group = queries.shape[1] // kv_heads
    me = lax.axis_index("ctx")
    if (shards == kv_heads == group == 8 and here == 2 and rand_blocks.shape[2] == 3
            and global_blocks.shape[0] == 2):
        return fused(queries, out_grad, keys, values, rand_blocks, global_blocks, shards)
    kv_here = jnp.stack([keys.transpose(1, 0, 2), values.transpose(1, 0, 2)], axis=1)
    kv = lax.all_gather(kv_here, "ctx", axis=0)
    rand_all = lax.all_gather(rand_blocks, "ctx", axis=0, tiled=True)
    bias = row_bias(rand_all, global_blocks, me * here, here, block_count, kv_heads)
    output, query_grad, parts = local_attention(queries, out_grad, kv, bias)
    sums = lax.psum_scatter(parts, "ctx", scatter_dimension=0, tiled=False)
    grads = sums.transpose(1, 2, 0, 3)
    return output, query_grad, grads[0], grads[1]


def solution(mesh):
    split = P(("dp", "ctx"), None, None)
    return jax.shard_map(
        functools.partial(body, mesh.shape["ctx"]),
        mesh=mesh,
        in_specs=(split, split, split, split, split, P("dp")),
        out_specs=(split, split, split, split),
        check_vma=False,
    )
```

time: 89 us -> 85.7 us (0.963)
  local copies, waits for them, and re-layouts: 7.72 us -> 4.04 us
  Pallas kernels: 79.7 us -> 80.8 us
    unnamed x11 -> x4, local copies, waits for them, and re-layouts: 6.74 us -> 4.04 us
    pallas_call x1, Pallas kernels: 79.7 us -> 80.8 us  [fused(): pl.pallas_call(fused_kernel, in_specs=[vmem, smem, vmem, vmem, anywhere,...]
where the time goes in v1:
time: 85.7 us; the launch traced here: 85.5 us
  Pallas kernels  80.8 us (94%)
  local copies, waits for them, and re-layouts  4.04 us (5%)
    pallas_call x1, Pallas kernels, fused(): pl.pallas_call(fused_kernel, in_specs=[vmem, smem, vmem, vmem, anywhere,...  80.8 us
    unnamed x4, local copies, waits for them, and re-layouts  4.04 us

profile of v1, /device:TPU:0, one launch (start us, length us, event | category | flops | bytes accessed | tf_op | source)
XLA Modules:
  0.0 85.5 jit_solution(12403778189523819420)
XLA Ops:
  0.6 80.8 %fused.1 = (bf16[128,64,128]{2,1,0:T(8,128)(2,1)S(1)}, bf16[128,64,128]{2,1,0:T(8,128)(2,1)S(1)}, bf16[128,8,128]{2,1,0:T(8,128)(2,1)S(1)}, bf16[128,8,128]{2,1,0:T(8,128)(2,1)S(1)}) custom-call(s32[3,8,16]{2,1,0:T(8,128)} %bitcast.1, s32[2]{0:T(128)} %glob_in.1, bf16[128,8,128]{2,1,0:T(8,128)(2,1)} %k_in.1, bf16[128,8,128]{2,1,0:T(8,128)(2,1)} %v_in.1, ...), custom_call_target="tpu_custom_call" | custom-call | tf_op jit(solution)/shard_map/fused/pallas_call | solution.py:608
  81.5 1.3 %copy.14 = bf16[128,64,128]{2,1,0:T(8,128)(2,1)} copy(bf16[128,64,128]{2,1,0:T(8,128)(2,1)S(1)} %get-tuple-element.4) | data formatting | bytes 4194304
  82.8 0.7 copy.16
  83.5 0.7 copy.17
  84.2 1.3 %copy.15 = bf16[128,64,128]{2,1,0:T(8,128)(2,1)} copy(bf16[128,64,128]{2,1,0:T(8,128)(2,1)S(1)} %get-tuple-element.5) | data formatting | bytes 4194304

commit v2 on v1

--- a/solution.py
+++ b/solution.py
@@ -11,6 +11,7 @@
 BLK = 64
 NT = (((1,), (1,)), ((), ()))
 NN = (((1,), (0,)), ((), ()))
+HIDDEN = -1e30
 
 
 def dot(left, right, dims=NN):
@@ -162,9 +163,9 @@
 def fused_kernel(
     rand_in, glob_in, k_in, v_in, q_hbm, g_hbm, out_ref, dq_ref, dk_ref, dv_ref,
     grads_ref, q_buf, g_buf, kv_buf, part_buf, sib_in, right_in, left_in, right_out, left_out,
-    ids_out, ids_buf, bias_buf, s_buf, e_buf, ds_buf, vt_buf, kt_buf, qt_buf, gt_buf,
+    ids_out, ids_buf, mark_buf, e_buf, ds_buf, vt_buf, kt_buf, qt_buf, gt_buf,
     q_sem, g_sem,
-    ids_send, sib_send, fwd_send, back_send, pair_send, right_send, left_send,
+    ids_send, sib_send, fwd_send, back_send, far_send, pair_send, right_send, left_send,
     ids_recv, sib_recv, kv_recv, pair_recv, right_recv, left_recv,
 ):
     heads, _, chips, _, shard_tokens, width = kv_buf.shape
@@ -224,10 +225,13 @@
     def pair_move(h, w):
         return send(part_buf.at[h, w, 1 - core], sib_in.at[h, w], pair_send, pair_recv.at[h, w], pair)
 
-    def side_move(side, h, w, zd):
-        if side == 0:
-            return send(right_out.at[h, w, zd], right_in.at[h, w, zd], right_send, right_recv.at[h, w, zd], ahead)
-        return send(left_out.at[h, w, zd], left_in.at[h, w, zd], left_send, left_recv.at[h, w, zd], behind)
+    def side_move(side, h, zd, w=None):
+        out, arrived = (right_out, right_in) if side == 0 else (left_out, left_in)
+        sems = (right_send, right_recv) if side == 0 else (left_send, left_recv)
+        at, slot = (h, zd), h
+        if w is not None:
+            at, slot = (h, zd, w), h + w
+        return send(out.at[at], arrived.at[at], sems[0], sems[1].at[slot, zd], ahead if side == 0 else behind)
 
     def head_columns(ref, h):
         return ref.at[:, pl.ds(pl.multiple_of(h * group, group), group), :]
@@ -262,6 +266,17 @@
                 ids_out[to, b * slots + k:b * slots + k + 1] = picks[spot:spot + 1]
     ids_buf[me] = ids_out[me]
 
+    length = shards * shard_tokens
+    spot = lax.broadcasted_iota(jnp.int32, (length, width), 0)
+    spot_lane, spot_chip = spot // lane_keys, spot % lane_keys // shard_tokens
+    spot_block = (spot_chip * 2 + spot_lane) * here + spot % shard_tokens // BLK
+    column = lax.broadcasted_iota(jnp.int32, (length, width), 1)
+    ones = jnp.logical_and(column >= block_count, column < block_count + 3)
+    mark_buf[...] = jnp.logical_or(column == spot_block, ones).astype(jnp.float32).astype(jnp.bfloat16)
+    vt_buf[width:, :] = jnp.ones((16, length), jnp.bfloat16)
+    qt_buf[width:, :] = jnp.zeros((width, rows), jnp.bfloat16)
+    gt_buf[width:, :] = jnp.zeros((width, rows), jnp.bfloat16)
+
     pl.semaphore_wait(barrier, shards - 1)
 
     def own_right(h):
@@ -277,19 +292,33 @@
     def own_sib(h):
         sib_kv(h, z).start()
 
-    def arrive(h, distance):
-        for zz in range(chips):
-            @pl.when(jnp.logical_and(z == zz, h < heads))
-            def _(zz=zz):
-                for origin in (zz - distance, zz + distance):
-                    if origin < 0 or origin > last:
-                        continue
-                    kv_move(h, origin, fwd_send, pair).wait_recv()
-                    if origin < zz < last:
-                        right_kv(h, origin).start()
-                    if 0 < zz < origin:
-                        left_kv(h, origin).start()
-                    sib_kv(h, origin).start()
+    ends = jnp.logical_or(z == 0, z == last)
+    middle = jnp.logical_not(ends)
+
+    def landed(h, origin):
+        kv_move(h, origin, fwd_send, pair).wait_recv()
+
+    def end_arrive(h, distance):
+        origin = jnp.where(z == 0, distance, last - distance)
+        landed(h, origin)
+        sib_kv(h, origin).start()
+
+    def near_arrive(h):
+        landed(h, z - 1)
+        right_kv(h, z - 1).start()
+        sib_kv(h, z - 1).start()
+        landed(h, z + 1)
+        left_kv(h, z + 1).start()
+        sib_kv(h, z + 1).start()
+
+    def far_origin():
+        return jnp.where(z == 1, last, 0)
+
+    def far_arrive(h):
+        origin = far_origin()
+        landed(h, origin)
+        kv_move(h, origin, far_send, jnp.where(z == 1, behind, ahead)).start()
+        sib_kv(h, origin).start()
 
     def over(low, high, step):
         def run(h, carry):
@@ -297,37 +326,44 @@
             return carry
         lax.fori_loop(low, high, run, 0)
 
-    def combined(h, w, zd):
-        return part_buf[h, w, core, zd].astype(jnp.float32) + sib_in[h, w, zd].astype(jnp.float32)
-
-    def reduce(rank, h, w):
+    def combined(h, zd, w=None):
+        at = slice(None) if w is None else w
+        return part_buf[h, at, core, zd].astype(jnp.float32) + sib_in[h, at, zd].astype(jnp.float32)
+
+    def reduce(rank, h, w=None, only=None):
         for side in range(2):
             zz = rank if side == 0 else last - rank
-            targets = range(last, zz, -1) if side == 0 else range(zz)
+            targets = list(range(last, zz, -1) if side == 0 else range(zz))
+            if only is not None:
+                targets = targets[only:only + 1]
             out, arrived = (right_out, right_in) if side == 0 else (left_out, left_in)
 
-            @pl.when(jnp.logical_and(z == zz, h >= 0))
+            @pl.when(z == zz)
             def _(side=side, targets=targets, out=out, arrived=arrived):
                 for zd in targets:
-                    total = combined(h, w, zd)
+                    at = (h, zd) if w is None else (h, zd, w)
+                    total = combined(h, zd, w)
                     if rank > 0:
-                        side_move(side, h, w, zd).wait_recv()
-                        total = total + arrived[h, w, zd].astype(jnp.float32)
-                    out[h, w, zd] = total.astype(jnp.bfloat16)
-                    side_move(side, h, w, zd).start()
-
-    def finish(h, w):
+                        side_move(side, h, zd, w).wait_recv()
+                        total = total + arrived[at].astype(jnp.float32)
+                    out[at] = total.astype(jnp.bfloat16)
+                    side_move(side, h, zd, w).start()
+
+    def finish(h, w=None):
         for zz in range(chips):
             @pl.when(z == zz)
             def _(zz=zz):
-                total = combined(h, w, zz)
+                at = (h, zz) if w is None else (h, zz, w)
+                total = combined(h, zz, w)
                 if zz > 0:
-                    side_move(0, h, w, zz).wait_recv()
-                    total = total + right_in[h, w, zz].astype(jnp.float32)
+                    side_move(0, h, zz, w).wait_recv()
+                    total = total + right_in[at].astype(jnp.float32)
                 if zz < last:
-                    side_move(1, h, w, zz).wait_recv()
-                    total = total + left_in[h, w, zz].astype(jnp.float32)
-                grads_ref[h, w] = total.T.astype(jnp.bfloat16)
+                    side_move(1, h, zz, w).wait_recv()
+                    total = total + left_in[at].astype(jnp.float32)
+                for which in range(2) if w is None else (w,):
+                    piece = total[which] if w is None else total
+                    grads_ref[h, which] = piece.T.astype(jnp.bfloat16)
 
     def compute(h, hooks):
         load_q(h).wait()
@@ -342,9 +378,9 @@
             live = (away <= 2) | (key_ids == glob_in[0]) | (key_ids == glob_in[1])
             for k in range(slots):
                 live = live | (key_float == ids[b * slots + k:b * slots + k + 1])
-            bias = jnp.where(live, 0.0, -jnp.inf).astype(jnp.float32)
-            for block in range(block_count):
-                bias_buf[b * block_count + block] = jnp.broadcast_to(bias[block:block + 1], (8, lanes))
+            bias = jnp.where(live, 0.0, HIDDEN).astype(jnp.float32).astype(jnp.bfloat16)
+            half = rows // here
+            qt_buf[width:width + block_count, b * half:(b + 1) * half] = jnp.concatenate([bias] * (half // lanes), axis=1)
 
         def key_rows(which, c):
             lane, zz = c * chunk // lane_keys, c * chunk % lane_keys // shard_tokens
@@ -363,54 +399,57 @@
             block = turned.T.reshape(tile_tokens, group, width)
             ref[r * tile_tokens:(r + 1) * tile_tokens, pl.ds(pl.multiple_of(h * group, group), group), :] = block
 
-        tops, totals, deltas = {}, {}, {}
+        tops = {}
 
         def turn_keys(which, ref):
             for c in range(chunks):
-                ref[:, keys_at(c)] = key_rows(which, c).T
+                ref[:width, keys_at(c)] = key_rows(which, c).T
+
+        def marked(which, at):
+            spot = at.start
+            keys = kv_buf[h, spot // lane_keys, spot % lane_keys // shard_tokens, which, pl.ds(spot % shard_tokens, 128)]
+            return jnp.concatenate([keys, mark_buf[at]], axis=1)
+
+        def slabs(size):
+            return [slice(at, at + size) for at in range(0, length, size)]
 
         def scores(r):
-            qt = turned_rows(q_buf, r)
-            qt_buf[:, columns(r)] = qt
-            b = r * tile // (rows // here)
+            qt_buf[:width, columns(r)] = turned_rows(q_buf, r)
+            right = qt_buf[:, columns(r)]
             top = None
-            for c in range(chunks):
-                lane, zz = c * chunk // lane_keys, c * chunk % lane_keys // shard_tokens
-                s = dot(key_rows(0, c), qt)
-                for j in range(chunk // BLK):
-                    block = ((zz + j // here) * 2 + lane) * here + j % here
-                    bias = bias_buf[b * block_count + block]
-                    bias = jnp.concatenate([bias] * (tile // lanes), axis=1)
-                    piece = s[j * BLK:(j + 1) * BLK].reshape(BLK // 8, 8, tile) + bias[None]
-                    at = c * chunk + j * BLK
-                    s_buf[at:at + BLK, columns(r)] = piece.reshape(BLK, tile)
-                    high = jnp.max(piece, axis=0)
-                    top = high if top is None else jnp.maximum(top, high)
+            for at in slabs(128):
+                s = dot(marked(0, at), right)
+                high = jnp.max(s.reshape(128 // 8, 8, tile), axis=0)
+                top = high if top is None else jnp.maximum(top, high)
             tops[r] = jnp.max(top, axis=0, keepdims=True) * to_log2
 
         def weights(r):
-            total = jnp.zeros((8, tile), jnp.float32)
-            for c in range(chunks):
-                e = jnp.exp2(s_buf[keys_at(c), columns(r)] * to_log2 - tops[r])
-                total = total + jnp.sum(e.reshape(chunk // 8, 8, tile), axis=0)
-                e_buf[keys_at(c), columns(r)] = e.astype(jnp.bfloat16)
-            totals[r] = jnp.sum(total, axis=0, keepdims=True)
+            right = qt_buf[:, columns(r)]
+            for at in slabs(128):
+                e = jnp.exp2(dot(marked(0, at), right) * to_log2 - tops[r])
+                e_buf[at, columns(r)] = e.astype(jnp.bfloat16)
 
         def outputs(r):
             out_t = dot(vt_buf[...], e_buf[:, columns(r)])
-            inverse = 1.0 / totals[r]
-            out16 = (out_t * inverse).astype(jnp.bfloat16)
+            inverse = 1.0 / out_t[width:width + 1]
+            out16 = (out_t[:width] * inverse).astype(jnp.bfloat16)
             gt = turned_rows(g_buf, r).astype(jnp.float32)
-            deltas[r] = jnp.sum(gt * out16.astype(jnp.float32), axis=0, keepdims=True) * inverse
-            gt_buf[:, columns(r)] = (gt * inverse).astype(jnp.bfloat16)
+            rest = jnp.sum(gt * out16.astype(jnp.float32), axis=0, keepdims=True) * -inverse
+            gt_buf[:width, columns(r)] = (gt * inverse).astype(jnp.bfloat16)
+            level = lax.broadcasted_iota(jnp.int32, (16, tile), 0)
+            split = jnp.zeros((16, tile), jnp.float32)
+            for k in range(3):
+                part = rest.astype(jnp.bfloat16).astype(jnp.float32)
+                split = jnp.where(level == k, part, split)
+                rest = rest - part
+            gt_buf[width + block_count:width + block_count + 16, columns(r)] = split.astype(jnp.bfloat16)
             put_rows(out_ref, r, out16)
 
         def score_grads(r):
-            gt = gt_buf[:, columns(r)]
-            for c in range(chunks):
-                dp = dot(key_rows(1, c), gt)
-                e = e_buf[keys_at(c), columns(r)].astype(jnp.float32)
-                ds_buf[keys_at(c), columns(r)] = (e * (dp - deltas[r])).astype(jnp.bfloat16)
+            right = gt_buf[:, columns(r)]
+            for at in slabs(128):
+                dp = dot(marked(1, at), right).astype(jnp.bfloat16)
+                ds_buf[at, columns(r)] = e_buf[at, columns(r)] * dp
 
         def query_grads(r):
             dq_t = dot(kt_buf[...], ds_buf[:, columns(r)]) * factor
@@ -420,7 +459,7 @@
             left, right = ((qt_buf, ds_buf), (gt_buf, e_buf))[w]
             for zz in range(0, chips, 2):
                 at = pl.ds(pl.multiple_of(lane * lane_keys + zz * shard_tokens, chunk), chunk)
-                grad = dot(left[...], right[at], NT)
+                grad = dot(left[:width], right[at], NT)
                 if w == 0:
                     grad = grad * factor
                 grad = grad.astype(jnp.bfloat16)
@@ -434,7 +473,6 @@
         scores(2)
         weights(1)
         outputs(0)
-        hooks[0]()
         scores(3)
         weights(2)
         outputs(1)
@@ -442,22 +480,17 @@
         weights(3)
         outputs(2)
         outputs(3)
-        hooks[1]()
+        hooks[0]()
         key_grads(1 - core, 1)
-        score_grads(0)
-        score_grads(1)
         pair_move(h, 1).start()
-        hooks[2]()
-        score_grads(2)
-        score_grads(3)
+        for r in range(tiles):
+            score_grads(r)
         key_grads(1 - core, 0)
         pair_move(h, 0).start()
-        hooks[3]()
         key_grads(core, 1)
         key_grads(core, 0)
         for r in range(tiles):
             query_grads(r)
-        hooks[4]()
 
     def lead(rank, t):
         return jnp.where(rank == 0, heads, jnp.minimum(jnp.where(rank == 1, 3 + 2 * t, 2 + t), heads))
@@ -473,20 +506,34 @@
     for k in range(1, shards):
         send_ids(k).start()
     each_head(start_loads)
-    arrive(0, 1)
+
+    @pl.when(middle)
+    def _():
+        near_arrive(0)
+
+    @pl.when(ends)
+    def _():
+        end_arrive(0, 1)
     over(1, lead(z, 0), own_right)
     over(1, lead(last - z, 0), own_left)
-    for distance in range(2, chips):
-        arrive(0, distance)
-    ends = jnp.logical_or(z == 0, z == last)
-    middle = jnp.logical_not(ends)
 
     @pl.when(middle)
     def _():
-        arrive(1, 1)
+        far_arrive(0)
+        near_arrive(1)
+
+    @pl.when(ends)
+    def _():
+        end_arrive(0, 2)
+        end_arrive(0, 3)
 
     for k in range(1, shards):
         got_ids(k).wait_recv()
+
+    final = heads - 1
+
+    def near_done(t):
+        return jnp.minimum(jnp.minimum(2 + 2 * t, 4 + t), heads)
 
     def slot(t, carry):
         over(lead(z, t), lead(z, t + 1), own_right)
@@ -496,76 +543,54 @@
         def _():
             own_sib(t + 3)
 
+        @pl.when(jnp.logical_and(middle, t == 1))
+        def _():
+            far_arrive(2)
+
         send(kv_buf.at[t, 1 - core], kv_buf.at[t, 1 - core], sib_send, sib_recv.at[t], pair).wait_recv()
 
-        def end_arrive(distance):
-            @pl.when(ends)
-            def _():
-                arrive(t + 1, distance)
-
-        def middle_arrive(*events):
-            for when, h, distance in events:
-                @pl.when(jnp.logical_and(middle, when))
-                def _(h=h, distance=distance):
-                    arrive(h, distance)
-
-        def caught(rank_lag):
-            low = jnp.where(t == heads - 2, 0, t - rank_lag)
-            return low, jnp.where(t < heads - 2, low, t - rank_lag + 1)
-
-        def far(w, rank_lag):
-            low, high = caught(rank_lag)
-            over(low, high, lambda h: reduce(2, h, w))
-
-        def hook0():
+        def hook():
             @pl.when(t > 0)
             def _():
+                pair_move(t - 1, 1).wait_recv()
                 pair_move(t - 1, 0).wait_recv()
-                reduce(0, t - 1, 0)
-            end_arrive(1)
-            middle_arrive((t == 0, 2, 1), (t == 0, 1, 2))
-
-        def hook1():
-            reduce(1, t - 1, 1)
-            far(0, 2)
-            end_arrive(2)
-            middle_arrive((t == 1, 4, 1), (t == 3, 7, 1))
-
-        def hook2():
-            end_arrive(3)
-            middle_arrive((t == 2, 6, 1), (t > 0, t + 2, 2))
-
-        def hook3():
-            middle_arrive((t == 0, 3, 1))
-
-        def hook4():
-            pair_move(t, 1).wait_recv()
-            reduce(0, t, 1)
-            reduce(1, t - 1, 0)
-            far(1, 1)
-            middle_arrive((t == 0, 2, 2), (t == 1, 5, 1))
-
-        compute(t, [hook0, hook1, hook2, hook3, hook4])
+                reduce(0, t - 1)
+
+            @pl.when(t > 1)
+            def _():
+                reduce(1, t - 2)
+
+            low = jnp.where(t == final - 1, 0, t - 3)
+            over(low, jnp.where(t < final - 1, low, t - 2), lambda h: reduce(2, h))
+
+            @pl.when(jnp.logical_and(ends, t < final))
+            def _():
+                for distance in range(1, chips):
+                    end_arrive(t + 1, distance)
+
+            @pl.when(middle)
+            def _():
+                over(near_done(t), near_done(t + 1), near_arrive)
+                far = jnp.where(t == 0, 1, t + 2)
+                over(far, jnp.minimum(far + 1, heads), far_arrive)
+
+        compute(t, [hook])
         return carry
 
     lax.fori_loop(0, heads, slot, 0)
 
-    final = heads - 1
-
-    def finish_both(h):
-        finish(h, 1)
-        finish(h, 0)
-
-    reduce(2, final - 1, 0)
-    reduce(1, final, 1)
-    reduce(2, final, 1)
+    reduce(1, final - 1)
+    reduce(2, final - 2)
+    reduce(2, final - 1)
+    pair_move(final, 1).wait_recv()
+    reduce(0, final, 1, 0)
     pair_move(final, 0).wait_recv()
-    reduce(0, final, 0)
-    over(0, 2, finish_both)
-    reduce(1, final, 0)
-    over(2, 5, finish_both)
-    reduce(2, final, 0)
-    over(5, heads, finish_both)
+    for rank, w, only in ((0, 0, 0), (0, 1, 1), (0, 0, 1), (0, 1, 2), (0, 0, 2),
+                          (1, 1, 0), (1, 0, 0), (2, 1, 0), (1, 1, 1), (2, 0, 0), (1, 0, 1)):
+        reduce(rank, final, w, only)
+    over(0, final, finish)
+    finish(final, 1)
+    finish(final, 0)
 
     for which, ref in enumerate((dk_ref, dv_ref)):
         turned = jnp.swapaxes(grads_ref[:, which].astype(jnp.float32), 0, 1)
@@ -577,15 +602,23 @@
     drained(ids_out.at[pl.ds(1, shards - 1)], ids_send)
     drained(kv_buf.at[:, 0], sib_send)
     drained(sib_in, pair_send)
+    @pl.when(middle)
+    def _():
+        drained(kv_buf.at[:, 0, pl.ds(0, 2)], fwd_send)
+        drained(kv_buf.at[:, 0, pl.ds(0, 2)], back_send)
+        drained(kv_buf.at[:, 0, 0], far_send)
+
     for zz in range(chips):
         @pl.when(z == zz)
         def _(zz=zz):
+            if zz == 0:
+                drained(kv_buf.at[:, 0, 0], fwd_send)
+            if zz == last:
+                drained(kv_buf.at[:, 0, 0], back_send)
             if zz < last:
-                drained(kv_buf.at[:, 0, pl.ds(0, zz + 1)], fwd_send)
-                drained(right_out.at[:, :, pl.ds(0, last - zz)], right_send)
+                drained(right_out.at[:, pl.ds(0, last - zz)], right_send)
             if zz > 0:
-                drained(kv_buf.at[:, 0, pl.ds(0, chips - zz)], back_send)
-                drained(left_out.at[:, :, pl.ds(0, zz)], left_send)
+                drained(left_out.at[:, pl.ds(0, zz)], left_send)
 
 
 def fused(queries, out_grad, keys, values, rand_blocks, global_blocks, shards):
@@ -604,7 +637,8 @@
     dma = pltpu.SemaphoreType.DMA
     piece = (2, tokens, width)
     block = pltpu.VMEM((kv_heads, tokens, group, width), bf16)
-    hop = pltpu.VMEM((kv_heads, 2, chips, width, tokens), bf16)
+    hop = pltpu.VMEM((kv_heads, chips, 2, width, tokens), bf16)
+    gift = pltpu.VMEM((kv_heads, 2, chips, width, tokens), bf16)
     results = pl.pallas_call(
         fused_kernel,
         in_specs=[vmem, smem, vmem, vmem, anywhere, anywhere],
@@ -620,23 +654,23 @@
             pltpu.VMEM((kv_heads, 2, chips) + piece, bf16),
             pltpu.VMEM((kv_heads, 2, 2, chips, width, tokens), bf16),
         ]
-        + [hop] * 5
+        + [gift]
+        + [hop] * 4
         + [
             pltpu.VMEM((shards, 8, 128), f32),
             pltpu.VMEM((shards, 8, 128), f32),
-            pltpu.VMEM((here * blocks, 8, 128), f32),
-            pltpu.VMEM((length, rows), f32),
+            pltpu.VMEM((length, 128), bf16),
             pltpu.VMEM((length, rows), bf16),
             pltpu.VMEM((length, rows), bf16),
+            pltpu.VMEM((width + 16, length), bf16),
             pltpu.VMEM((width, length), bf16),
-            pltpu.VMEM((width, length), bf16),
-            pltpu.VMEM((width, rows), bf16),
-            pltpu.VMEM((width, rows), bf16),
+            pltpu.VMEM((2 * width, rows), bf16),
+            pltpu.VMEM((2 * width, rows), bf16),
         ]
         + [dma((kv_heads,))] * 2
-        + [dma] * 7
+        + [dma] * 8
         + [dma((shards,)), dma((kv_heads,)), dma((kv_heads, chips)), dma((kv_heads, 2))]
-        + [dma((kv_heads, 2, chips))] * 2,
+        + [dma((kv_heads + 1, chips))] * 2,
         compiler_params=pltpu.CompilerParams(
             collective_id=0, has_side_effects=True, vmem_limit_bytes=50 * 1024 * 1024
         ),

time: 85.7 us -> 79.2 us (0.924)
  Pallas kernels: 80.8 us -> 74.3 us
    pallas_call x1, Pallas kernels: 80.8 us -> 74.3 us  [fused(): pl.pallas_call(fused_kernel, in_specs=[vmem, smem, vmem, vmem, anywhere,...]
where the time goes in v2:
time: 79.2 us; the launch traced here: 79 us
  Pallas kernels  74.3 us (94%)
  local copies, waits for them, and re-layouts  4.04 us (5%)
    pallas_call x1, Pallas kernels, fused(): pl.pallas_call(fused_kernel, in_specs=[vmem, smem, vmem, vmem, anywhere,...  74.3 us
    unnamed x4, local copies, waits for them, and re-layouts  4.04 us

profile of v2, /device:TPU:0, one launch (start us, length us, event | category | flops | bytes accessed | tf_op | source)
XLA Modules:
  0.0 79.0 jit_solution(17682011790983656021)
XLA Ops:
  0.6 74.3 %fused.1 = (bf16[128,64,128]{2,1,0:T(8,128)(2,1)S(1)}, bf16[128,64,128]{2,1,0:T(8,128)(2,1)S(1)}, bf16[128,8,128]{2,1,0:T(8,128)(2,1)S(1)}, bf16[128,8,128]{2,1,0:T(8,128)(2,1)S(1)}) custom-call(s32[3,8,16]{2,1,0:T(8,128)} %bitcast.1, s32[2]{0:T(128)} %glob_in.1, bf16[128,8,128]{2,1,0:T(8,128)(2,1)} %k_in.1, bf16[128,8,128]{2,1,0:T(8,128)(2,1)} %v_in.1, ...), custom_call_target="tpu_custom_call" | custom-call | tf_op jit(solution)/shard_map/fused/pallas_call | solution.py:642
  75.0 1.3 %copy.14 = bf16[128,64,128]{2,1,0:T(8,128)(2,1)} copy(bf16[128,64,128]{2,1,0:T(8,128)(2,1)S(1)} %get-tuple-element.4) | data formatting | bytes 4194304
  76.3 0.7 copy.16
  77.0 0.7 copy.17
  77.7 1.3 %copy.15 = bf16[128,64,128]{2,1,0:T(8,128)(2,1)} copy(bf16[128,64,128]{2,1,0:T(8,128)(2,1)S(1)} %get-tuple-element.5) | data formatting | bytes 4194304

commit v3 on v2

--- a/solution.py
+++ b/solution.py
@@ -12,6 +12,8 @@
 NT = (((1,), (1,)), ((), ()))
 NN = (((1,), (0,)), ((), ()))
 HIDDEN = -1e30
+COARSE = jnp.float8_e4m3fn
+COARSE_MAX = 448.0
 
 
 def dot(left, right, dims=NN):
@@ -163,7 +165,7 @@
 def fused_kernel(
     rand_in, glob_in, k_in, v_in, q_hbm, g_hbm, out_ref, dq_ref, dk_ref, dv_ref,
     grads_ref, q_buf, g_buf, kv_buf, part_buf, sib_in, right_in, left_in, right_out, left_out,
-    ids_out, ids_buf, mark_buf, e_buf, ds_buf, vt_buf, kt_buf, qt_buf, gt_buf,
+    ids_out, ids_buf, mark_buf, coarse_k, coarse_q, e_buf, ds_buf, vt_buf, kt_buf, qt_buf, gt_buf,
     q_sem, g_sem,
     ids_send, sib_send, fwd_send, back_send, far_send, pair_send, right_send, left_send,
     ids_recv, sib_recv, kv_recv, pair_recv, right_recv, left_recv,
@@ -208,18 +210,21 @@
         origin = lax.rem(me + k, shards)
         return send(ids_out.at[origin], ids_buf.at[origin], ids_send, ids_recv.at[origin], origin)
 
-    def kv_move(h, origin, send_sem, to):
-        spot = kv_buf.at[h, core, origin]
-        return send(spot, spot, send_sem, kv_recv.at[h, origin], to)
-
-    def right_kv(h, origin):
-        return kv_move(h, origin, fwd_send, ahead)
-
-    def left_kv(h, origin):
-        return kv_move(h, origin, back_send, behind)
-
-    def sib_kv(h, origin):
-        spot = kv_buf.at[h, core, origin]
+    def kv_spot(h, origin, w):
+        return kv_buf.at[h, core, origin] if w is None else kv_buf.at[h, core, origin, w]
+
+    def kv_move(h, origin, send_sem, to, w=None):
+        spot = kv_spot(h, origin, w)
+        return send(spot, spot, send_sem, kv_recv.at[heads if w == 1 else h, origin], to)
+
+    def right_kv(h, origin, w=None):
+        return kv_move(h, origin, fwd_send, ahead, w)
+
+    def left_kv(h, origin, w=None):
+        return kv_move(h, origin, back_send, behind, w)
+
+    def sib_kv(h, origin, w=None):
+        spot = kv_spot(h, origin, w)
         return send(spot, spot, sib_send, sib_recv.at[h], pair)
 
     def pair_move(h, w):
@@ -273,21 +278,23 @@
     column = lax.broadcasted_iota(jnp.int32, (length, width), 1)
     ones = jnp.logical_and(column >= block_count, column < block_count + 3)
     mark_buf[...] = jnp.logical_or(column == spot_block, ones).astype(jnp.float32).astype(jnp.bfloat16)
+    coarse_k[:, width:] = jnp.where(column == spot_block, COARSE_MAX, 0.0).astype(COARSE)
+    coarse_q[width:, :] = jnp.zeros((width, rows), jnp.float32).astype(COARSE)
     vt_buf[width:, :] = jnp.ones((16, length), jnp.bfloat16)
     qt_buf[width:, :] = jnp.zeros((width, rows), jnp.bfloat16)
     gt_buf[width:, :] = jnp.zeros((width, rows), jnp.bfloat16)
 
     pl.semaphore_wait(barrier, shards - 1)
 
-    def own_right(h):
+    def own_right(h, w=None):
         @pl.when(z < last)
         def _():
-            right_kv(h, z).start()
-
-    def own_left(h):
+            right_kv(h, z, w).start()
+
+    def own_left(h, w=None):
         @pl.when(z > 0)
         def _():
-            left_kv(h, z).start()
+            left_kv(h, z, w).start()
 
     def own_sib(h):
         sib_kv(h, z).start()
@@ -295,30 +302,27 @@
     ends = jnp.logical_or(z == 0, z == last)
     middle = jnp.logical_not(ends)
 
-    def landed(h, origin):
-        kv_move(h, origin, fwd_send, pair).wait_recv()
-
-    def end_arrive(h, distance):
+    def landed(h, origin, w=None):
+        kv_move(h, origin, fwd_send, pair, w).wait_recv()
+
+    def end_arrive(h, distance, w=None):
         origin = jnp.where(z == 0, distance, last - distance)
-        landed(h, origin)
-        sib_kv(h, origin).start()
-
-    def near_arrive(h):
-        landed(h, z - 1)
-        right_kv(h, z - 1).start()
-        sib_kv(h, z - 1).start()
-        landed(h, z + 1)
-        left_kv(h, z + 1).start()
-        sib_kv(h, z + 1).start()
-
-    def far_origin():
-        return jnp.where(z == 1, last, 0)
-
-    def far_arrive(h):
-        origin = far_origin()
-        landed(h, origin)
-        kv_move(h, origin, far_send, jnp.where(z == 1, behind, ahead)).start()
-        sib_kv(h, origin).start()
+        landed(h, origin, w)
+        sib_kv(h, origin, w).start()
+
+    def near_arrive(h, w=None):
+        landed(h, z - 1, w)
+        right_kv(h, z - 1, w).start()
+        sib_kv(h, z - 1, w).start()
+        landed(h, z + 1, w)
+        left_kv(h, z + 1, w).start()
+        sib_kv(h, z + 1, w).start()
+
+    def far_arrive(h, w=None):
+        origin = jnp.where(z == 1, last, 0)
+        landed(h, origin, w)
+        kv_move(h, origin, far_send, jnp.where(z == 1, behind, ahead), w).start()
+        sib_kv(h, origin, w).start()
 
     def over(low, high, step):
         def run(h, carry):
@@ -381,6 +385,9 @@
             bias = jnp.where(live, 0.0, HIDDEN).astype(jnp.float32).astype(jnp.bfloat16)
             half = rows // here
             qt_buf[width:width + block_count, b * half:(b + 1) * half] = jnp.concatenate([bias] * (half // lanes), axis=1)
+            hide = jnp.where(live, 0.0, -COARSE_MAX).astype(jnp.float32)
+            hide = jnp.concatenate([hide, jnp.zeros((32 - block_count, lanes), jnp.float32)], axis=0).astype(COARSE)
+            coarse_q[width:width + 32, b * half:(b + 1) * half] = jnp.concatenate([hide] * (half // lanes), axis=1)
 
         def key_rows(which, c):
             lane, zz = c * chunk // lane_keys, c * chunk % lane_keys // shard_tokens
@@ -413,13 +420,18 @@
         def slabs(size):
             return [slice(at, at + size) for at in range(0, length, size)]
 
+        def coarse_keys():
+            for c in range(chunks):
+                coarse_k[keys_at(c), :width] = key_rows(0, c).astype(jnp.float32).astype(COARSE)
+
         def scores(r):
-            qt_buf[:width, columns(r)] = turned_rows(q_buf, r)
-            right = qt_buf[:, columns(r)]
+            qt = turned_rows(q_buf, r)
+            qt_buf[:width, columns(r)] = qt
+            coarse_q[:width, columns(r)] = qt.astype(jnp.float32).astype(COARSE)
+            right = coarse_q[:, columns(r)]
             top = None
             for at in slabs(128):
-                s = dot(marked(0, at), right)
-                high = jnp.max(s.reshape(128 // 8, 8, tile), axis=0)
+                high = jnp.max(dot(coarse_k[at], right).reshape(128 // 8, 8, tile), axis=0)
                 top = high if top is None else jnp.maximum(top, high)
             tops[r] = jnp.max(top, axis=0, keepdims=True) * to_log2
 
@@ -467,6 +479,7 @@
                     part_buf[h, w, lane, zz + j] = grad[:, j * shard_tokens:(j + 1) * shard_tokens]
 
         turn_keys(1, vt_buf)
+        coarse_keys()
         scores(0)
         scores(1)
         weights(0)
@@ -480,11 +493,11 @@
         weights(3)
         outputs(2)
         outputs(3)
-        hooks[0]()
         key_grads(1 - core, 1)
         pair_move(h, 1).start()
         for r in range(tiles):
             score_grads(r)
+        hooks[0]()
         key_grads(1 - core, 0)
         pair_move(h, 0).start()
         key_grads(core, 1)
@@ -499,33 +512,41 @@
         load_q(h).start()
         load_g(h).start()
 
-    own_right(0)
-    own_left(0)
+    for w in range(2):
+        own_right(0, w)
+        own_left(0, w)
     for h in range(3):
         own_sib(h)
     for k in range(1, shards):
         send_ids(k).start()
+
+    @pl.when(z == 0)
+    def _():
+        over(1, heads, own_right)
+
+    @pl.when(z == last)
+    def _():
+        over(1, heads, own_left)
     each_head(start_loads)
 
     @pl.when(middle)
     def _():
-        near_arrive(0)
+        near_arrive(0, 0)
+        near_arrive(0, 1)
+        right_kv(1, z).start()
+        left_kv(1, z).start()
+        far_arrive(0, 0)
+        far_arrive(0, 1)
+        near_arrive(1)
+
+    over(jnp.where(ends, heads, 2), lead(z, 0), own_right)
+    over(jnp.where(ends, heads, 2), lead(last - z, 0), own_left)
 
     @pl.when(ends)
     def _():
-        end_arrive(0, 1)
-    over(1, lead(z, 0), own_right)
-    over(1, lead(last - z, 0), own_left)
-
-    @pl.when(middle)
-    def _():
-        far_arrive(0)
-        near_arrive(1)
-
-    @pl.when(ends)
-    def _():
-        end_arrive(0, 2)
-        end_arrive(0, 3)
+        for distance in range(1, chips):
+            end_arrive(0, distance, 0)
+            end_arrive(0, distance, 1)
 
     for k in range(1, shards):
         got_ids(k).wait_recv()
@@ -660,6 +681,8 @@
             pltpu.VMEM((shards, 8, 128), f32),
             pltpu.VMEM((shards, 8, 128), f32),
             pltpu.VMEM((length, 128), bf16),
+            pltpu.VMEM((length, 2 * width), COARSE),
+            pltpu.VMEM((2 * width, rows), COARSE),
             pltpu.VMEM((length, rows), bf16),
             pltpu.VMEM((length, rows), bf16),
             pltpu.VMEM((width + 16, length), bf16),
@@ -669,14 +692,36 @@
         ]
         + [dma((kv_heads,))] * 2
         + [dma] * 8
-        + [dma((shards,)), dma((kv_heads,)), dma((kv_heads, chips)), dma((kv_heads, 2))]
+        + [dma((shards,)), dma((kv_heads,)), dma((kv_heads + 1, chips)), dma((kv_heads, 2))]
         + [dma((kv_heads + 1, chips))] * 2,
         compiler_params=pltpu.CompilerParams(
             collective_id=0, has_side_effects=True, vmem_limit_bytes=50 * 1024 * 1024
         ),
         name="fused",
     )(rand_blocks.transpose(2, 0, 1), global_blocks, keys, values, queries, out_grad)
-    return results
+    return settle(results)
+
+
+def settle(arrays):
+    count = len(arrays)
+
+    def kernel(*refs):
+        copies = [pltpu.make_async_copy(refs[i], refs[count + i], refs[2 * count].at[i]) for i in range(count)]
+        for copy in copies:
+            copy.start()
+        for copy in copies:
+            copy.wait()
+
+    anywhere = pl.BlockSpec(memory_space=pl.ANY)
+    return pl.pallas_call(
+        kernel,
+        in_specs=[pl.BlockSpec(memory_space=pltpu.VMEM)] * count,
+        out_specs=[pl.BlockSpec(memory_space=pltpu.HBM)] * count,
+        out_shape=[jax.ShapeDtypeStruct(a.shape, a.dtype) for a in arrays],
+        scratch_shapes=[pltpu.SemaphoreType.DMA((count,))],
+        compiler_params=pltpu.CompilerParams(vmem_limit_bytes=1 << 20),
+        name="settle",
+    )(*[pltpu.with_memory_space_constraint(a, pltpu.VMEM) for a in arrays])
 
 
 def body(shards, queries, keys, values, out_grad, rand_blocks, global_blocks):

time: 79.2 us -> 75.6 us (0.955)
  local copies, waits for them, and re-layouts: 4.04 us -> 0 us
    unnamed x4 -> x0, local copies, waits for them, and re-layouts: 4.04 us -> none
    pallas_call x0 -> x1, Pallas kernels: none -> 2.2 us  [settle(): pl.pallas_call(kernel, in_specs=[pl.BlockSpec(memory_space=pltpu.VMEM)] *...]
    pallas_call x1, Pallas kernels: 74.3 us -> 72.6 us  [fused(): pl.pallas_call(fused_kernel, in_specs=[vmem, smem, vmem, vmem, anywhere,...]
where the time goes in v3:
time: 75.6 us; the launch traced here: 75.4 us
  Pallas kernels  74.8 us (99%)
    pallas_call x1, Pallas kernels, fused(): pl.pallas_call(fused_kernel, in_specs=[vmem, smem, vmem, vmem, anywhere,...  72.6 us
    pallas_call x1, Pallas kernels, settle(): pl.pallas_call(kernel, in_specs=[pl.BlockSpec(memory_space=pltpu.VMEM)] *...  2.2 us

profile of v3, /device:TPU:0, one launch (start us, length us, event | category | flops | bytes accessed | tf_op | source)
XLA Modules:
  0.0 75.4 jit_solution(6175599730842070135)
XLA Ops:
  0.6 72.6 %fused.1 = (bf16[128,64,128]{2,1,0:T(8,128)(2,1)S(1)}, bf16[128,64,128]{2,1,0:T(8,128)(2,1)S(1)}, bf16[128,8,128]{2,1,0:T(8,128)(2,1)S(1)}, bf16[128,8,128]{2,1,0:T(8,128)(2,1)S(1)}) custom-call(s32[3,8,16]{2,1,0:T(8,128)} %bitcast.1, s32[2]{0:T(128)} %glob_in.1, bf16[128,8,128]{2,1,0:T(8,128)(2,1)} %k_in.1, bf16[128,8,128]{2,1,0:T(8,128)(2,1)} %v_in.1, ...), custom_call_target="tpu_custom_call" | custom-call | tf_op jit(solution)/shard_map/fused/pallas_call | solution.py:663
  73.2 2.2 %settle.1 = (bf16[128,64,128]{2,1,0:T(8,128)(2,1)}, bf16[128,64,128]{2,1,0:T(8,128)(2,1)}, bf16[128,8,128]{2,1,0:T(8,128)(2,1)}, bf16[128,8,128]{2,1,0:T(8,128)(2,1)}) custom-call(bf16[128,64,128]{2,1,0:T(8,128)(2,1)S(1)} %get-tuple-element.8.refs_0_, bf16[128,64,128]{2,1,0:T(8,128)(2,1)S(1)} %get-tuple-element.9.refs_1_, ...), custom_call_target="tpu_custom_call" | custom-call | tf_op jit(solution)/shard_map/settle/pallas_call | solution.py:716

commit v4 on v3

--- a/solution.py
+++ b/solution.py
@@ -413,8 +413,9 @@
                 ref[:width, keys_at(c)] = key_rows(which, c).T
 
         def marked(which, at):
-            spot = at.start
-            keys = kv_buf[h, spot // lane_keys, spot % lane_keys // shard_tokens, which, pl.ds(spot % shard_tokens, 128)]
+            size, spot = at.stop - at.start, at.start
+            lane, zz = spot // lane_keys, spot % lane_keys // shard_tokens
+            keys = kv_buf[h, lane, zz:zz + size // shard_tokens, which].reshape(size, width)
             return jnp.concatenate([keys, mark_buf[at]], axis=1)
 
         def slabs(size):
@@ -430,14 +431,14 @@
             coarse_q[:width, columns(r)] = qt.astype(jnp.float32).astype(COARSE)
             right = coarse_q[:, columns(r)]
             top = None
-            for at in slabs(128):
-                high = jnp.max(dot(coarse_k[at], right).reshape(128 // 8, 8, tile), axis=0)
+            for at in slabs(512):
+                high = jnp.max(dot(coarse_k[at], right).reshape(512 // 8, 8, tile), axis=0)
                 top = high if top is None else jnp.maximum(top, high)
             tops[r] = jnp.max(top, axis=0, keepdims=True) * to_log2
 
         def weights(r):
             right = qt_buf[:, columns(r)]
-            for at in slabs(128):
+            for at in slabs(512):
                 e = jnp.exp2(dot(marked(0, at), right) * to_log2 - tops[r])
                 e_buf[at, columns(r)] = e.astype(jnp.bfloat16)
 
@@ -459,7 +460,7 @@
 
         def score_grads(r):
             right = gt_buf[:, columns(r)]
-            for at in slabs(128):
+            for at in slabs(512):
                 dp = dot(marked(1, at), right).astype(jnp.bfloat16)
                 ds_buf[at, columns(r)] = e_buf[at, columns(r)] * dp
 
@@ -571,6 +572,17 @@
         send(kv_buf.at[t, 1 - core], kv_buf.at[t, 1 - core], sib_send, sib_recv.at[t], pair).wait_recv()
 
         def hook():
+            @pl.when(jnp.logical_and(ends, t < final))
+            def _():
+                for distance in range(1, chips):
+                    end_arrive(t + 1, distance)
+
+            @pl.when(middle)
+            def _():
+                far = jnp.where(t == 0, 1, t + 2)
+                over(far, jnp.minimum(far + 1, heads), far_arrive)
+                over(near_done(t), near_done(t + 1), near_arrive)
+
             @pl.when(t > 0)
             def _():
                 pair_move(t - 1, 1).wait_recv()
@@ -583,17 +595,6 @@
 
             low = jnp.where(t == final - 1, 0, t - 3)
             over(low, jnp.where(t < final - 1, low, t - 2), lambda h: reduce(2, h))
-
-            @pl.when(jnp.logical_and(ends, t < final))
-            def _():
-                for distance in range(1, chips):
-                    end_arrive(t + 1, distance)
-
-            @pl.when(middle)
-            def _():
-                over(near_done(t), near_done(t + 1), near_arrive)
-                far = jnp.where(t == 0, 1, t + 2)
-                over(far, jnp.minimum(far + 1, heads), far_arrive)
 
         compute(t, [hook])
         return carry

time: 75.6 us -> 73.1 us (0.967)
  Pallas kernels: 74.8 us -> 72.3 us
    pallas_call x1, Pallas kernels: 72.6 us -> 70.1 us  [fused(): pl.pallas_call(fused_kernel, in_specs=[vmem, smem, vmem, vmem, anywhere,...]
where the time goes in v4:
time: 73.1 us; the launch traced here: 72.9 us
  Pallas kernels  72.3 us (99%)
    pallas_call x1, Pallas kernels, fused(): pl.pallas_call(fused_kernel, in_specs=[vmem, smem, vmem, vmem, anywhere,...  70.1 us
    pallas_call x1, Pallas kernels, settle(): pl.pallas_call(kernel, in_specs=[pl.BlockSpec(memory_space=pltpu.VMEM)] *...  2.2 us

profile of v4, /device:TPU:0, one launch (start us, length us, event | category | flops | bytes accessed | tf_op | source)
XLA Modules:
  0.0 72.9 jit_solution(15347991296354541756)
XLA Ops:
  0.6 70.1 %fused.1 = (bf16[128,64,128]{2,1,0:T(8,128)(2,1)S(1)}, bf16[128,64,128]{2,1,0:T(8,128)(2,1)S(1)}, bf16[128,8,128]{2,1,0:T(8,128)(2,1)S(1)}, bf16[128,8,128]{2,1,0:T(8,128)(2,1)S(1)}) custom-call(s32[3,8,16]{2,1,0:T(8,128)} %bitcast.1, s32[2]{0:T(128)} %glob_in.1, bf16[128,8,128]{2,1,0:T(8,128)(2,1)} %k_in.1, bf16[128,8,128]{2,1,0:T(8,128)(2,1)} %v_in.1, ...), custom_call_target="tpu_custom_call" | custom-call | tf_op jit(solution)/shard_map/fused/pallas_call | solution.py:664
  70.7 2.2 %settle.1 = (bf16[128,64,128]{2,1,0:T(8,128)(2,1)}, bf16[128,64,128]{2,1,0:T(8,128)(2,1)}, bf16[128,8,128]{2,1,0:T(8,128)(2,1)}, bf16[128,8,128]{2,1,0:T(8,128)(2,1)}) custom-call(bf16[128,64,128]{2,1,0:T(8,128)(2,1)S(1)} %get-tuple-element.8.refs_0_, bf16[128,64,128]{2,1,0:T(8,128)(2,1)S(1)} %get-tuple-element.9.refs_1_, ...), custom_call_target="tpu_custom_call" | custom-call | tf_op jit(solution)/shard_map/settle/pallas_call | solution.py:717
